TPU v7x, 256 devices: a whole 4x4x8 slice. The times are simulated.
256 devices in a mesh: dp: 4 (over y_hi, core), seq: 8 (over z), head: 8 (over x, y_lo).
Axes of the slice: x: 4, y: 4 (y_hi: 2, y_lo: 2; y = y_hi * 2 + y_lo), z: 8, core: 2. Of those that a mesh axis runs over, the one named last changes fastest.
Arguments:
- tokens: bfloat16 [4, 8192, 512], P('dp', ('seq', 'head')), may hold values from -800 to 800
- bin_ids: int32 [4, 8192], P('dp'), may hold values from 0 to 127, never falling along the last dimension, each value on 1 to 256 neighbouring positions
- pattern: int32 [4, 64, 9], P('dp'), may hold values from 0 to 63, as said below
- w_qkv: bfloat16 [512, 1536], replicated, may hold values from -3.2 to 3.2
- w_out: bfloat16 [512, 512], replicated, may hold values from -5 to 5
- head_bias: float32 [8], replicated, may hold values from -3 to 400
- grad_output: bfloat16 [4, 8192, 512], P('dp', ('seq', 'head')), may hold values from -6 to 6
Outputs:
- output: bfloat16 [4, 8192, 512], P('dp', ('seq', 'head'))
- grad_tokens: bfloat16 [4, 8192, 512], P('dp', ('seq', 'head'))
- grad_w_qkv: float32 [512, 1536], P(None, 'head')
- grad_w_out: float32 [512, 512], P('head')
Inputs may be any that keep to these rules, and one draw needn't show every extreme that they name: `pattern`: row i of sequence b lists (i + o) mod 64 for the 9 offsets o of sequence b, in the same order in every row: 0, 1, -1, then distinct a from 2 to 31, then their negatives. So block J is in row I exactly when I is in row J. `bin_ids`: bin numbers never fall along a sequence.
All inputs are finite; a program needn't handle non-finite values.
Results may differ from a plain program's by a relative error of at most 0.01.
Values may be sent and summed in bfloat16 or wider, within the bound.
A program may use at most 64 MiB of HBM per device.

v0:
```python
import math

import jax
import jax.numpy as jnp
from jax import lax
from jax.sharding import PartitionSpec as P

D = 512
HEADS = 8
HD = 64
BLK = 128
NNZ = 9


EPSILON = 1e-05


def normalize(token_rows):
    widened = token_rows.astype(jnp.float32)
    spread = jnp.sqrt(jnp.mean(widened * widened, axis=-1, keepdims=True) + EPSILON)
    return (widened / spread, spread)


def query_scores(query_blk, key_blk, bin_query, bin_key, bias_local, factor):
    raw_scores = jnp.einsum(
        "gqhe,gnkhe->ghqnk", query_blk, key_blk, preferred_element_type=jnp.float32
    )
    same_bin = (bin_query[:, None, :, None, None] == bin_key[:, None, None, :, :]).astype(
        jnp.float32
    )
    scores = raw_scores * factor + bias_local[None, :, None, None, None] * same_bin
    return scores.reshape(scores.shape[0], scores.shape[1], scores.shape[2], -1)


def body(tokens, bin_ids, pattern, w_qkv, w_out, head_bias, grad_output):
    tok_rows = tokens.shape[1]
    head_parts = lax.axis_size("head")
    local_heads = HEADS // head_parts
    seq_rows = tok_rows * head_parts
    seq_length = bin_ids.shape[1]
    blocks_all = seq_length // BLK
    local_blocks = seq_rows // BLK
    group_size = math.gcd(local_blocks, 4)
    group_count = local_blocks // group_size
    factor = 1.0 / math.sqrt(HD)
    seq_pos = lax.axis_index("seq")
    head_pos = lax.axis_index("head")
    first_block = seq_pos * local_blocks
    key_lists = lax.dynamic_slice_in_dim(pattern[0], first_block, local_blocks, 0)
    bin_table = bin_ids[0].reshape(blocks_all, BLK)
    bin_local = lax.dynamic_slice_in_dim(bin_table, first_block, local_blocks, 0)
    bias_local = lax.dynamic_slice_in_dim(head_bias, head_pos * local_heads, local_heads, 0)

    def grouped(array):
        return array.reshape((group_count, group_size) + array.shape[1:])

    normed, spread = normalize(tokens[0])
    hidden = normed.astype(jnp.bfloat16)
    packed = jnp.dot(hidden, w_qkv, preferred_element_type=jnp.float32).astype(jnp.bfloat16)
    packed = packed.reshape(tok_rows, HEADS, 3 * HD)
    packed_heads = lax.all_to_all(packed, "head", split_axis=1, concat_axis=0, tiled=True)
    queries = packed_heads[:, :, :HD]
    pair_local = packed_heads[:, :, HD:]
    pair_all = lax.all_gather(pair_local, "seq", axis=0, tiled=True)
    pair_table = pair_all.reshape(blocks_all, BLK, local_heads, 2 * HD)
    query_blocks = queries.reshape(local_blocks, BLK, local_heads, HD)

    def forward_group(entries):
        query_blk, key_rows, bin_query = entries
        pair_blk = jnp.take(pair_table, key_rows, axis=0)
        bin_key = jnp.take(bin_table, key_rows, axis=0)
        scores = query_scores(query_blk, pair_blk[..., :HD], bin_query, bin_key, bias_local, factor)
        row_max = jnp.max(scores, axis=-1, keepdims=True)
        log_total = row_max + jnp.log(jnp.sum(jnp.exp(scores - row_max), axis=-1, keepdims=True))
        probs = jnp.exp(scores - log_total).astype(jnp.bfloat16)
        value_flat = pair_blk[..., HD:].reshape(group_size, NNZ * BLK, local_heads, HD)
        attended = jnp.einsum(
            "ghqm,gmhe->gqhe", probs, value_flat, preferred_element_type=jnp.float32
        )
        return (attended.astype(jnp.bfloat16), log_total[..., 0])

    attended, log_blocks = lax.map(
        forward_group, (grouped(query_blocks), grouped(key_lists), grouped(bin_local))
    )
    attended_heads = attended.reshape(seq_rows, local_heads, HD)
    log_blocks = log_blocks.reshape(local_blocks, local_heads, BLK)
    attended_tok = lax.all_to_all(
        attended_heads, "head", split_axis=0, concat_axis=1, tiled=True
    ).reshape(tok_rows, D)
    result = jnp.dot(attended_tok, w_out, preferred_element_type=jnp.float32).astype(jnp.bfloat16)
    grad_rows = grad_output[0]
    grad_att = jnp.dot(grad_rows, w_out.T, preferred_element_type=jnp.float32).astype(jnp.bfloat16)
    grad_heads = lax.all_to_all(
        grad_att.reshape(tok_rows, HEADS, HD), "head", split_axis=1, concat_axis=0, tiled=True
    )
    delta_rows = jnp.sum(
        grad_heads.astype(jnp.float32) * attended_heads.astype(jnp.float32), axis=-1
    )
    delta_blocks = delta_rows.reshape(local_blocks, BLK, local_heads).swapaxes(1, 2)
    grad_blocks = grad_heads.reshape(local_blocks, BLK, local_heads, HD)

    def query_core(entries):
        query_blk, grad_blk, log_blk, delta_blk, key_rows, bin_query = entries
        pair_blk = jnp.take(pair_table, key_rows, axis=0)
        bin_key = jnp.take(bin_table, key_rows, axis=0)
        scores = query_scores(query_blk, pair_blk[..., :HD], bin_query, bin_key, bias_local, factor)
        probs = jnp.exp(scores - log_blk[..., None])
        value_flat = pair_blk[..., HD:].reshape(group_size, NNZ * BLK, local_heads, HD)
        key_flat = pair_blk[..., :HD].reshape(group_size, NNZ * BLK, local_heads, HD)
        grad_prob = jnp.einsum(
            "gqhe,gmhe->ghqm", grad_blk, value_flat, preferred_element_type=jnp.float32
        )
        grad_score = (probs * (grad_prob - delta_blk[..., None]) * factor).astype(jnp.bfloat16)
        grad_query = jnp.einsum(
            "ghqm,gmhe->gqhe", grad_score, key_flat, preferred_element_type=jnp.float32
        )
        return (grad_query.astype(jnp.bfloat16), grad_score, probs)

    query_entries = (
        grouped(query_blocks),
        grouped(grad_blocks),
        grouped(log_blocks),
        grouped(delta_blocks),
        grouped(key_lists),
        grouped(bin_local),
    )

    def scatter_step(carried, entries):
        query_blk, grad_blk = (entries[0], entries[1])
        key_rows = entries[4]
        grad_query, grad_score, probs = query_core(entries)
        key_part = jnp.einsum(
            "ghqm,gqhe->gmhe", grad_score, query_blk, preferred_element_type=jnp.float32
        )
        value_part = jnp.einsum(
            "ghqm,gqhe->gmhe",
            probs.astype(jnp.bfloat16),
            grad_blk,
            preferred_element_type=jnp.float32,
        )
        both_parts = jnp.concatenate([key_part, value_part], axis=-1)
        both_parts = both_parts.reshape(group_size * NNZ, BLK, local_heads, 2 * HD)
        carried = carried.at[key_rows.reshape(-1)].add(both_parts)
        return (carried, grad_query)

    empty_sum = jnp.zeros((blocks_all, BLK, local_heads, 2 * HD), jnp.float32)
    pair_sums, grad_queries = lax.scan(scatter_step, empty_sum, query_entries)
    own_pairs = lax.psum_scatter(
        pair_sums.reshape(seq_length, local_heads, 2 * HD), "seq", scatter_dimension=0, tiled=True
    )
    grad_pairs = own_pairs.astype(jnp.bfloat16)
    grad_packed_heads = jnp.concatenate(
        [grad_queries.reshape(seq_rows, local_heads, HD), grad_pairs], axis=-1
    )
    grad_packed = lax.all_to_all(
        grad_packed_heads, "head", split_axis=0, concat_axis=1, tiled=True
    ).reshape(tok_rows, 3 * D)
    grad_hidden = jnp.dot(grad_packed, w_qkv.T, preferred_element_type=jnp.float32)
    inner = jnp.mean(grad_hidden * normed, axis=-1, keepdims=True)
    grad_input = ((grad_hidden - normed * inner) / spread).astype(jnp.bfloat16)
    local_qkv = jnp.einsum("td,tc->dc", hidden, grad_packed, preferred_element_type=jnp.float32)
    local_out = jnp.einsum("td,tc->dc", grad_rows, attended_tok, preferred_element_type=jnp.float32)
    total_qkv, total_out = lax.psum((local_qkv, local_out), ("dp", "seq", "head"))
    own_qkv = lax.dynamic_slice_in_dim(
        total_qkv, head_pos * local_heads * 3 * HD, local_heads * 3 * HD, 1
    )
    own_out = lax.dynamic_slice_in_dim(total_out, head_pos * local_heads * HD, local_heads * HD, 1)
    return (result[None], grad_input[None], own_qkv, own_out.T)


def solution(mesh):
    return jax.shard_map(
        body,
        mesh=mesh,
        in_specs=(
            P("dp", ("seq", "head"), None),
            P("dp", None),
            P("dp", None, None),
            P(),
            P(),
            P(),
            P("dp", ("seq", "head"), None),
        ),
        out_specs=(
            P("dp", ("seq", "head"), None),
            P("dp", ("seq", "head"), None),
            P(None, "head"),
            P("head", None),
        ),
        check_vma=False,
    )
```

profile of v0, /device:TPU:1, one launch (start us, length us, event | category | flops | bytes accessed | tf_op | source)
XLA Modules:
  0.0 557.6 jit_solution(6286347255980764140)
XLA Ops:
  7.2 1.1 fusion.34
  9.0 1.4 convolution_convert_fusion.1
  10.6 12.8 %all_to_all.63 = bf16[128,8,192]{0,2,1:T(8,128)(2,1)S(1)} all-to-all(bf16[128,8,192]{0,2,1:T(8,128)(2,1)S(1)} %bitcast.271), channel_id=1, replica_groups=mesh['dp'=4,'seq'=8,'head'=8] {'head'}, dimensions={1} | all-to-all | bytes 786432 | tf_op jit(solution)/shard_map/all_to_all | solution.py:61
  25.3 3.4 all-to-all-start.2
  29.7 34.8 %all-gather.2.cloned.1.call-done = bf16[8192,1,128]{0,2,1:T(8,128)(2,1)} async-done(((bf16[1024,1,128]{0,2,1:T(8,128)(2,1)}), bf16[8192,1,128]{0,2,1:T(8,128)(2,1)}) %all-gather.2.cloned.1.call-update) | async-done | bytes 2097168 | tf_op jit(solution)/shard_map/all_gather | solution.py:64
  64.5 4.1 copy.119
  69.3 40.3 %while.24 = (s32[]{:T(128)}, bf16[2,4,128,1,64]{2,4,1,3,0:T(8,128)(2,1)}, f32[2,4,1,128]{3,1,2,0:T(4,128)}, s32[2,4,9]{2,1,0:T(4,128)S(1)}, bf16[64,128,1,128]{3...) while((s32[]{:T(128)}, ...), condition=%wide.region_4.7_spmd, body=%wide.region_1.6_spmd.sunk | while | flops 156931296 | bytes 39141280 | solution.py:82
  70.6 3.4 gather_fusion
  74.1 1.7 copy.151
  75.9 1.0 copy-done.4
  77.8 3.7 fusion.80
  81.5 1.4 copy-done.2
  83.3 3.1 copy.153
  86.4 2.3 fusion.81
  90.8 3.4 gather_fusion
  94.2 1.7 copy.151
  96.1 1.0 copy-done.4
  98.0 3.7 fusion.80
  101.7 1.4 copy-done.2
  103.5 3.1 copy.153
  106.6 2.3 fusion.81
  111.2 2.5 broadcast_in_dim.54
  113.7 86.0 %while.25 = (s32[]{:T(128)}, f32[64,128,1,128]{3,1,0,2:T(8,128)}, bf16[2,4,128,1,64]{2,4,1,3,0:T(8,128)(2,1)}, s32[2,4,9]{2,1,0:T(4,128)S(1)}, bf16[2,4,128,1,64...) while((s32[]{:T(128)}, f32[64,128,1,128]{3,1,0,2:T(8,128)}, ...), condition=%wide.region_8.11_spmd, body=%wide.region_6.10_spmd.sunk | while | flops 385783744 | bytes 64560684 | solution.py:147
  116.4 2.4 gather_fusion.3
  118.8 1.4 copy.154
  120.2 1.4 broadcast_select_fusion.11
  122.6 1.4 copy.156
  124.0 1.5 reshape.431
  125.5 2.5 copy.158
  128.0 2.1 reshape.432
  130.2 4.2 select_add_fusion.3
  134.4 3.1 copy.155
  137.5 2.5 fusion.94
  142.0 1.6 pad_maximum_fusion.3
  143.6 3.1 copy.157
  146.7 10.1 %scatter_fusion = f32[64,128,128]{2,1,0:T(8,128)} fusion(f32[64,128,128]{2,1,0:T(8,128)} %bitcast.263, s32[36]{0:T(128)S(1)} %copy-done.24, f32[36,128,128]{2,1,0:T(8,128)} %bitcast.257), kind=kCustom, calls=%fused_computation.4.clone.1 | custom fusion | flops 589824 | bytes 7078032 | tf_op jit(solution)/shard_map/while/body/eval_jaxpr/scatter-add | solution.py:143
  159.5 2.4 gather_fusion.3
  161.9 1.4 copy.154
  163.3 1.4 broadcast_select_fusion.11
  165.7 1.4 copy.156
  167.1 1.5 reshape.431
  168.6 2.5 copy.158
  171.1 2.1 reshape.432
  173.3 4.2 select_add_fusion.3
  177.5 3.1 copy.155
  180.6 2.5 fusion.94
  185.1 1.6 pad_maximum_fusion.3
  186.7 3.1 copy.157
  189.8 9.9 %scatter_fusion = f32[64,128,128]{2,1,0:T(8,128)} fusion(f32[64,128,128]{2,1,0:T(8,128)} %bitcast.263, s32[36]{0:T(128)S(1)} %copy-done.24, f32[36,128,128]{2,1,0:T(8,128)} %bitcast.257), kind=kCustom, calls=%fused_computation.4.clone.1 | custom fusion | flops 589824 | bytes 7078032 | tf_op jit(solution)/shard_map/while/body/eval_jaxpr/scatter-add | solution.py:143
  201.7 2.3 reduce.9
  204.8 4.9 all-to-all-start.1
  210.1 47.4 %reduce-scatter.2.cloned.1.call-done = f32[1024,1,128]{2,1,0:T(1,128)} async-done(((f32[8192,1,128]{2,1,0:T(1,128)}), f32[1024,1,128]{2,1,0:T(1,128)}) %reduce-scatter.2.cloned.1.call-update) | async-done | bytes 524304 | tf_op jit(solution)/shard_map/reduce_scatter | solution.py:148
  257.5 1.4 convert_element_type.98
  258.9 2.0 pad_maximum_fusion.1
  260.9 4.1 reduce.10
  265.0 1.3 reshape.395
  266.3 4.9 all-to-all-start.3
  272.0 1.3 convolution_bitcast_fusion.2
  273.2 5.2 all-to-all-done.3
  280.0 2.3 fusion.38
  282.3 1.0 copy-done.7
  285.8 262.0 %all-reduce.3.cloned.1.call-done = (f32[512,1536]{0,1:T(8,128)}, f32[512,512]{0,1:T(8,128)}) async-done(((f32[512,1536]{0,1:T(8,128)}, f32[512,512]{0,1:T(8,128)}), (f32[512,1536]{0,1:T(8,128)}, f32[512,512]{0,1:T(8,128)})) %all-reduce.3.cloned.1.call-update) | async-done | bytes 4194320 | tf_op jit(solution)/shard_map/psum | solution.py:163
  547.7 1.8 constant_dynamic-slice_fusion.1
  549.5 1.6 dynamic-slice_bitcast_fusion.4
  (184 shorter events, 31.6 us)
Async XLA Ops:
  7.2 1.8 copy-start
  7.2 57.4 %all-gather.2.cloned.1.call-start = ((), (), s32[]{:S(2)}) async-start(), calls=%async_computation.5 | async-start | bytes 2359296 | tf_op jit(solution)/shard_map/all_gather | solution.py:64
  8.4 0.6 copy-start.26
  9.0 15.3 %copy-start.6 = (bf16[512,512]{1,0:T(8,128)(2,1)S(1)}, bf16[512,512]{1,0:T(8,128)(2,1)}, u32[]{:S(2)}) copy-start(bf16[512,512]{1,0:T(8,128)(2,1)} %param.19) | copy-start | bytes 1572868
  9.0 15.3 %copy-start.17 = (bf16[1,128,512]{2,1,0:T(8,128)(2,1)S(1)}, bf16[1,128,512]{2,1,0:T(8,128)(2,1)}, u32[]{:S(2)}) copy-start(bf16[1,128,512]{2,1,0:T(8,128)(2,1)} %param.21) | copy-start | bytes 393220
  10.3 18.4 %copy-start.25 = (s32[1,64,9]{1,0,2:T(1,128)S(1)}, s32[1,64,9]{1,0,2:T(1,128)}, u32[]{:S(2)}) copy-start(s32[1,64,9]{1,0,2:T(1,128)} %param.17) | copy-start | bytes 6916
  10.4 18.6 %copy-start.28 = (f32[8]{0:T(128)S(1)}, f32[8]{0:T(128)}, u32[]{:S(2)}) copy-start(f32[8]{0:T(128)} %param.20) | copy-start | bytes 100
  10.4 19.3 %copy-start.3 = (s32[1,8192]{1,0:T(1,128)S(1)}, s32[1,8192]{1,0:T(1,128)}, u32[]{:S(2)}) copy-start(s32[1,8192]{1,0:T(1,128)} %param.16) | copy-start | bytes 98308
  25.3 84.3 %all-to-all-start.2 = ((bf16[128,8,64]{0,2,1:T(8,128)(2,1)}), bf16[128,8,64]{0,2,1:T(8,128)(2,1)S(1)}, u32[]{:S(2)}, u32[]{:S(2)}) async-start(bf16[128,8,64]{0,2,1:T(8,128)(2,1)} %bitcast.50), calls=%async_computation.2 | async-start | bytes 262144 | tf_op jit(solution)/shard_map/all_to_all | solution.py:93
  28.7 228.8 %reduce-scatter.2.cloned.1.call-start = ((), (), s32[]{:S(2)}) async-start(), calls=%async_computation.6 | async-start | bytes 4718592 | tf_op jit(solution)/shard_map/reduce_scatter | solution.py:148
  75.9 1.0 copy-start.4
  77.0 0.8 copy-start.19
  77.8 5.4 copy-start.22
  81.5 1.4 copy-start.2
  83.3 3.2 copy-start.23
  83.3 3.1 copy-start.10
  88.8 0.7 copy-start.11
  96.1 1.0 copy-start.4
  97.1 0.8 copy-start.19
  98.0 5.4 copy-start.22
  101.6 1.4 copy-start.2
  103.4 3.2 copy-start.23
  103.4 3.1 copy-start.10
  108.9 0.7 copy-start.11
  113.7 2.6 copy-start.20
  113.7 6.5 %copy-start.8 = (bf16[2,4,128,1,64]{2,4,1,3,0:T(8,128)(2,1)}, bf16[2,4,128,1,64]{2,4,1,3,0:T(8,128)(2,1)S(1)}, u32[]{:S(2)}) copy-start(bf16[2,4,128,1,64]{2,4,1,3,0:T(8,128)(2,1)S(1)} %get-tuple-element.496) | copy-start | bytes 393220 | tf_op jit(solution)/shard_map/while
  137.5 2.5 copy-start.1
  140.0 1.1 copy-start.5
  140.0 1.1 copy-start.14
  140.0 1.6 copy-start.9
  141.7 1.9 copy-start.15
  143.6 3.1 copy-start.24
  146.7 10.1 %copy-start.21 = (f32[2,4,1,128]{3,1,2,0:T(4,128)S(1)}, f32[2,4,1,128]{3,1,2,0:T(4,128)}, u32[]{:S(2)}) copy-start(f32[2,4,1,128]{3,1,2,0:T(4,128)} %copy-done.20) | copy-start | bytes 12292 | tf_op jit(solution)/shard_map/while
  156.8 2.6 copy-start.20
  156.8 6.5 %copy-start.8 = (bf16[2,4,128,1,64]{2,4,1,3,0:T(8,128)(2,1)}, bf16[2,4,128,1,64]{2,4,1,3,0:T(8,128)(2,1)S(1)}, u32[]{:S(2)}) copy-start(bf16[2,4,128,1,64]{2,4,1,3,0:T(8,128)(2,1)S(1)} %get-tuple-element.496) | copy-start | bytes 393220 | tf_op jit(solution)/shard_map/while
  180.6 2.5 copy-start.1
  183.1 1.1 copy-start.5
  183.1 1.1 copy-start.14
  183.1 1.6 copy-start.9
  184.8 1.9 copy-start.15
  186.7 3.1 copy-start.24
  189.8 9.9 %copy-start.21 = (f32[2,4,1,128]{3,1,2,0:T(4,128)S(1)}, f32[2,4,1,128]{3,1,2,0:T(4,128)}, u32[]{:S(2)}) copy-start(f32[2,4,1,128]{3,1,2,0:T(4,128)} %copy-done.20) | copy-start | bytes 12292 | tf_op jit(solution)/shard_map/while
  199.7 0.9 copy-start.12
  200.6 9.1 %copy-start.16 = (bf16[2,4,128,1,64]{2,4,1,3,0:T(8,128)(2,1)S(1)}, bf16[2,4,128,1,64]{2,4,1,3,0:T(8,128)(2,1)}, u32[]{:S(2)}) copy-start(bf16[2,4,128,1,64]{2,4,1,3,0:T(8,128)(2,1)} %get-tuple-element.119) | copy-start | bytes 393220
  204.8 61.5 %all-to-all-start.1 = ((bf16[8,2,4096]{2,1,0:T(2,128)(2,1)}), bf16[8,2,4096]{2,1,0:T(2,128)(2,1)S(1)}, u32[]{:S(2)}, u32[]{:S(2)}) async-start(bf16[8,2,4096]{2,1,0:T(2,128)(2,1)} %reshape.393), calls=%async_computation.1 | async-start | bytes 262144 | tf_op jit(solution)/shard_map/all_to_all | solution.py:87
  260.9 11.1 %copy-start.18 = (bf16[1,128,512]{2,1,0:T(8,128)(2,1)S(1)}, bf16[1,128,512]{2,1,0:T(8,128)(2,1)}, u32[]{:S(2)}) copy-start(bf16[1,128,512]{2,1,0:T(8,128)(2,1)} %param.21) | copy-start | bytes 393220
  266.3 12.1 %all-to-all-start.3 = ((bf16[8,2,12288]{2,1,0:T(2,128)(2,1)}), bf16[8,2,12288]{2,1,0:T(2,128)(2,1)S(1)}, u32[]{:S(2)}, u32[]{:S(2)}) async-start(bf16[8,2,12288]{2,1,0:T(2,128)(2,1)} %reshape.395), calls=%async_computation.4 | async-start | bytes 786432 | tf_op jit(solution)/shard_map/all_to_all | solution.py:155
  271.2 276.5 %all-reduce.3.cloned.1.call-start = ((), (), s32[]{:S(2)}) async-start(), calls=%async_computation.7 | async-start | bytes 8388608 | tf_op jit(solution)/shard_map/psum | solution.py:163
  273.2 6.7 %copy-start.13 = (bf16[1,128,512]{2,1,0:T(8,128)(2,1)S(1)}, bf16[1,128,512]{2,1,0:T(8,128)(2,1)}, u32[]{:S(2)}) copy-start(bf16[1,128,512]{2,1,0:T(8,128)(2,1)} %param.15) | copy-start | bytes 393220
  273.2 6.7 %copy-start.27 = (f32[128]{0:T(128)S(1)}, f32[128]{0:T(128)}, u32[]{:S(2)}) copy-start(f32[128]{0:T(128)} %copy-done.26) | copy-start | bytes 1540
  282.3 1.0 copy-start.7
Sparse Core Ops, SparseCore 0:
  24.4 40.1 all-gather.1
  199.9 57.5 reduce-scatter.1
  282.4 265.2 all-reduce.2
where the time goes:
time: 560 us; the launch traced here: 558 us
  waiting for transfers between devices  349 us (62%)
  local copies, waits for them, and re-layouts  90.9 us (16%)
  other arithmetic  41.3 us (7%)
  matrix products  35.3 us (6%)
  between operations  14.1 us (3%)
  starting transfers between devices  13.3 us (2%)
  blocking collectives  12.8 us (2%)
    psum x1, waiting for transfers between devices, body(): lax.psum((local_qkv, local_out), ('dp', 'seq', 'head'))  262 us
    reduce_scatter x1, waiting for transfers between devices, body(): lax.psum_scatter(pair_sums.reshape(seq_length, local_heads, 2 * HD), 'seq...  47.4 us
    all_gather x1, waiting for transfers between devices, body(): pair_all = lax.all_gather(pair_local, 'seq', axis=0, tiled=True)  34.8 us
    scatter-add x2, other arithmetic, scatter_step(): carried = carried.at[key_rows.reshape(-1)].add(both_parts)  20 us
    dot_general x4, matrix products, query_scores(): jnp.einsum('gqhe,gnkhe->ghqnk', query_blk, key_blk, preferred_element_typ...  15.7 us
    all_to_all x1, blocking collectives, body(): lax.all_to_all(packed, 'head', split_axis=1, concat_axis=0, tiled=True)  12.8 us
    reshape x4, local copies, waits for them, and re-layouts, query_scores(): return scores.reshape(scores.shape[0], scores.shape[1], scores.shape[2], -1)  12.5 us
  transfers between devices with their start and end apart: 6, of which 4 were waited for; matrix products, arithmetic and copies ran while one was open for 10% of the time, Pallas kernels for 0%

commit v1 on v0

v1 whole, which is shorter than its diff:
```python
import functools
import math

import jax
import jax.numpy as jnp
from jax import lax
from jax.experimental import pallas as pl
from jax.experimental.pallas import tpu as pltpu
from jax.sharding import PartitionSpec as P

D = 512
HEADS = 8
HD = 64
BLK = 128
NNZ = 9
SPANS = 8
PER = 8
NB = SPANS * PER
EPSILON = 1e-05
LOG2E = math.log2(math.e)
MESH = pl.DeviceIdType.MESH
F32 = jnp.float32
BF16 = jnp.bfloat16


def dot_nn(a, b):
    return lax.dot_general(a, b, (((1,), (0,)), ((), ())), preferred_element_type=F32)


def dot_nt(a, b):
    return lax.dot_general(a, b, (((1,), (1,)), ((), ())), preferred_element_type=F32)


A_KV, A_QD, A_HID, A_GO, A_BQO, A_BKV, A_ST, A_RS0, A_RS1, A_AG0, A_AG1 = range(11)


def kernel(
    pat_ref, bias_ref, tok_ref, gout_ref, wqkv_ref, wout_ref, bins_ref,
    out_ref, gtok_ref, gqkv_ref, gwo_ref,
    gkv, gqd, hid, gog, skv, sqd, normed_ref, spread_ref,
    ycat, a2, sd, pd, stcol, strow, stg, binsf, binst,
    bqo, bkv, rqo, rkv, dtqo, dtkv,
    wpart, ars, arr, dpx, fin, att, gp,
    ss, rr, dps, dpr, zs, zr,
):
    dp = lax.axis_index("dp")
    s = lax.axis_index("seq")
    h = lax.axis_index("head")
    factor = 1.0 / math.sqrt(HD)
    c2 = factor * LOG2E

    def mod8(v):
        return lax.rem(v + 16, 8)

    def send(kind, d, axis, src, dst):
        peer = mod8((h if axis == "head" else s) + d)
        return pltpu.make_async_remote_copy(
            src_ref=src,
            dst_ref=dst,
            send_sem=ss.at[kind, d],
            recv_sem=rr.at[kind, d],
            device_id={axis: peer},
            device_id_type=MESH,
        )

    pending = []

    def start(copy):
        copy.start()
        pending.append(copy)
        return copy

    barrier = pltpu.get_barrier_semaphore()
    for d in range(1, 8):
        pl.semaphore_signal(barrier, inc=1, device_id={"head": mod8(h + d)}, device_id_type=MESH)
        pl.semaphore_signal(barrier, inc=1, device_id={"seq": mod8(s + d)}, device_id_type=MESH)
    for d in range(1, 4):
        pl.semaphore_signal(
            barrier, inc=1, device_id={"dp": lax.rem(dp + d, 4)}, device_id_type=MESH
        )

    lane = lax.broadcasted_iota(jnp.int32, (BLK, 2 * HD), 1)
    low = lane < HD

    def swap(x):
        return pltpu.roll(x, HD, 1)

    x = tok_ref[...].astype(F32)
    spread = jnp.sqrt(jnp.mean(x * x, axis=-1, keepdims=True) + EPSILON)
    normed = x / spread
    normed_ref[...] = normed
    spread_ref[...] = spread
    hidden = normed.astype(BF16)
    hid[h] = hidden
    gout = gout_ref[...]
    gog[h] = gout
    for g in range(HEADS // 2):
        t = dot_nn(hidden, wqkv_ref[:, g * 384 : (g + 1) * 384])
        u = dot_nt(gout, wout_ref[g * 128 : (g + 1) * 128, :])
        t0, t1, t2 = t[:, 0:128], t[:, 128:256], t[:, 256:384]
        st1 = swap(t1)
        skv[2 * g] = jnp.where(low, swap(t0), st1).astype(BF16)
        skv[2 * g + 1] = t2.astype(BF16)
        sqd[2 * g] = jnp.where(low, t0, swap(u)).astype(BF16)
        sqd[2 * g + 1] = jnp.where(low, st1, u).astype(BF16)
    gkv[PER * s + h] = skv[h]
    gqd[PER * s + h] = sqd[h]

    pl.semaphore_wait(barrier, 17)

    def a2a(kind, src_of, dst):
        return [start(send(kind, d, "head", src_of(mod8(h + d)), dst)) for d in range(1, 8)]

    c_kv = a2a(A_KV, lambda p: skv.at[p], gkv.at[PER * s + h])
    c_qd = a2a(A_QD, lambda p: sqd.at[p], gqd.at[PER * s + h])
    c_hid = a2a(A_HID, lambda p: hid.at[h], hid.at[h])
    c_go = a2a(A_GO, lambda p: gog.at[h], gog.at[h])

    binsf[...] = bins_ref[...].astype(F32)
    binst[...] = jnp.concatenate([binsf[...], jnp.zeros((BLK - NB, BLK), F32)], axis=0).T

    right, left = mod8(s + 1), mod8(s - 1)

    def hop(which, buf, way, t, c):
        span = mod8(s - t + 1) if way == 0 else mod8(s + t - 1)
        part = buf.at[pl.ds(PER * span + 4 * c, 4)]
        return pltpu.make_async_remote_copy(
            src_ref=part,
            dst_ref=part,
            send_sem=zs.at[which, way, t, c],
            recv_sem=zr.at[which, way, t, c],
            device_id={"seq": right if way == 0 else left},
            device_id_type=MESH,
        )

    def used(way, t, c):
        return t < 4 or c == way

    def first_hop(which, buf):
        return {(w, 1, c): start(hop(which, buf, w, 1, c)) for c in (0, 1) for w in (0, 1)}

    def next_hop(which, buf, table, t):
        for c in (0, 1):
            for w in (0, 1):
                table[w, t, c].wait_recv()
                if used(w, t + 1, c):
                    table[w, t + 1, c] = start(hop(which, buf, w, t + 1, c))

    def last_hop(table):
        for w in (0, 1):
            table[w, 4, w].wait_recv()

    for copy in c_kv:
        copy.wait_recv()
    z_kv = first_hop(0, gkv)
    for t in (1, 2, 3):
        next_hop(0, gkv, z_kv, t)
    for copy in c_qd:
        copy.wait_recv()
    z_qd = first_hop(1, gqd)
    last_hop(z_kv)

    bias2 = bias_ref[h] * LOG2E

    def gather(buf, row):
        for n in range(NNZ):
            ycat[n * BLK : (n + 1) * BLK, :] = buf[pat_ref[row, n]]

    def stack_halves(block):
        zero = jnp.zeros((BLK, 2 * HD), BF16)
        a2[0:BLK, :] = jnp.where(low, block, zero)
        a2[BLK : 2 * BLK, :] = jnp.where(low, zero, block)

    def own_bins(row):
        return jnp.sum(jnp.where(lane == row, binst[...], 0.0), axis=1, keepdims=True)

    def tile(n):
        return slice(n * BLK, (n + 1) * BLK)

    stcol[...] = jnp.zeros((BLK, BLK), F32)

    def query_block(i, carry):
        row = PER * s + i
        gather(gkv, row)
        stack_halves(gqd[row])
        sd[...] = dot_nt(a2[...], ycat[...])
        bin_col = own_bins(row)
        top = None
        for n in range(NNZ):
            bin_row = binsf[pl.ds(pat_ref[row, n], 1), :]
            v = sd[0:BLK, tile(n)] * c2 + jnp.where(bin_col == bin_row, bias2, 0.0)
            sd[0:BLK, tile(n)] = v
            top = v if top is None else jnp.maximum(top, v)
        m = jnp.max(top, axis=1, keepdims=True)
        total = jnp.zeros((BLK, BLK), F32)
        inner = jnp.zeros((BLK, BLK), F32)
        for n in range(NNZ):
            p = jnp.exp2(sd[0:BLK, tile(n)] - m)
            sd[0:BLK, tile(n)] = p
            total = total + p
            inner = inner + p * sd[BLK : 2 * BLK, tile(n)]
        total = jnp.sum(total, axis=1, keepdims=True)
        delta = jnp.sum(inner, axis=1, keepdims=True) / total
        for n in range(NNZ):
            p = sd[0:BLK, tile(n)]
            pd[0:BLK, tile(n)] = p.astype(BF16)
            pd[BLK : 2 * BLK, tile(n)] = (p * (sd[BLK : 2 * BLK, tile(n)] - delta)).astype(BF16)
        r = dot_nn(pd[...], ycat[...])
        inv = 1.0 / total
        both = jnp.where(low, r[BLK : 2 * BLK] * (inv * factor), r[0:BLK] * inv)
        bqo[i] = both.astype(BF16)
        dtqo[:, pl.ds(pl.multiple_of(i * BLK, BLK), BLK)] = both.T.astype(BF16)
        logs = m + jnp.log2(total)
        stcol[...] = jnp.where(
            lane == 2 * i, logs, jnp.where(lane == 2 * i + 1, delta, stcol[...])
        )
        return carry

    lax.fori_loop(0, PER, query_block, 0)

    strow[...] = stcol[...].T
    stg[pl.ds(pl.multiple_of(2 * PER * s, 16), 16), :] = strow[0:16, :]
    mine = stg.at[pl.ds(pl.multiple_of(2 * PER * s, 16), 16)]
    c_st = [start(send(A_ST, d, "seq", mine, mine)) for d in range(1, 8)]
    next_hop(1, gqd, z_qd, 1)
    rqo[h] = bqo[h]
    c_bqo = a2a(A_BQO, lambda p: bqo.at[p], rqo.at[h])
    next_hop(1, gqd, z_qd, 2)

    for copy in c_hid:
        copy.wait_recv()
    for copy in c_go:
        copy.wait_recv()
    hid_all = hid[...].reshape(PER * BLK, D)
    go_all = gog[...].reshape(PER * BLK, D)

    def reduce_send(k, part):
        wpart[k] = part
        for z in range(SPANS):
            ars[k, z] = part[16 * z : 16 * (z + 1), :].astype(BF16)
        return [
            start(send((A_RS0, A_RS1)[k], d, "seq", ars.at[k, mod8(s + d)], arr.at[k, s]))
            for d in range(1, 8)
        ]

    def reduce_dp(k, copies):
        total = wpart[k, pl.ds(pl.multiple_of(16 * s, 16), 16), :]
        for d, copy in zip(range(1, 8), copies):
            copy.wait_recv()
            total = total + arr[k, mod8(s - d)].astype(F32)
        dpx[k, dp] = total.astype(BF16)
        sent = []
        for d in range(1, 4):
            sent.append(
                start(
                    pltpu.make_async_remote_copy(
                        src_ref=dpx.at[k, dp],
                        dst_ref=dpx.at[k, dp],
                        send_sem=dps.at[k, d],
                        recv_sem=dpr.at[k, d],
                        device_id={"dp": lax.rem(dp + d, 4)},
                        device_id_type=MESH,
                    )
                )
            )
        return sent

    def reduce_gather(k, copies):
        for copy in copies:
            copy.wait_recv()
        total = dpx[k, 0].astype(F32)
        for q in range(1, 4):
            total = total + dpx[k, q].astype(F32)
        fin[k, s] = total.astype(BF16)
        return [
            start(send((A_AG0, A_AG1)[k], d, "seq", fin.at[k, s], fin.at[k, s]))
            for d in range(1, 8)
        ]

    part0 = jnp.concatenate(
        [dot_nn(dtqo[0:HD, :], hid_all), dot_nn(dtqo[HD : 2 * HD, :], go_all)], axis=0
    )
    next_hop(1, gqd, z_qd, 3)
    rs0 = reduce_send(0, part0)
    for copy in c_st:
        copy.wait_recv()
    last_hop(z_qd)

    def key_block(i, carry):
        row = PER * s + i
        gather(gqd, row)
        stack_halves(gkv[row])
        sd[...] = dot_nt(a2[...], ycat[...])
        bin_col = own_bins(row)
        for n in range(NNZ):
            other = pat_ref[row, n]
            bin_row = binsf[pl.ds(other, 1), :]
            log_row = stg[pl.ds(2 * other, 1), :]
            delta_row = stg[pl.ds(2 * other + 1, 1), :]
            v = sd[0:BLK, tile(n)] * c2 + jnp.where(bin_col == bin_row, bias2, 0.0)
            p = jnp.exp2(v - log_row)
            pd[0:BLK, tile(n)] = p.astype(BF16)
            pd[BLK : 2 * BLK, tile(n)] = (p * (sd[BLK : 2 * BLK, tile(n)] - delta_row)).astype(BF16)
        r = dot_nn(pd[...], ycat[...])
        both = jnp.where(low, r[BLK : 2 * BLK] * factor, r[0:BLK])
        bkv[i] = both.astype(BF16)
        dtkv[:, pl.ds(pl.multiple_of(i * BLK, BLK), BLK)] = both.T.astype(BF16)
        return carry

    lax.fori_loop(0, PER, key_block, 0)

    rkv[h] = bkv[h]
    c_bkv = a2a(A_BKV, lambda p: bkv.at[p], rkv.at[h])
    part1 = dot_nn(dtkv[...], hid[...].reshape(PER * BLK, D))
    rs1 = reduce_send(1, part1)
    dp0 = reduce_dp(0, rs0)

    for copy in c_bqo:
        copy.wait_recv()
    for g in range(HEADS // 2):
        even, odd = rqo[2 * g].astype(F32), rqo[2 * g + 1].astype(F32)
        att[:, g * 128 : (g + 1) * 128] = jnp.where(low, swap(even), odd).astype(BF16)
    out_ref[...] = dot_nn(att[...], wout_ref[...]).astype(BF16)
    dp1 = reduce_dp(1, rs1)
    ag0 = reduce_gather(0, dp0)

    for copy in c_bkv:
        copy.wait_recv()
    for g in range(HEADS // 2):
        qo_even, qo_odd = rqo[2 * g].astype(F32), rqo[2 * g + 1].astype(F32)
        kv_even = swap(rkv[2 * g].astype(F32))
        gp[:, g * 384 : g * 384 + 128] = jnp.where(low, qo_even, kv_even).astype(BF16)
        gp[:, g * 384 + 128 : g * 384 + 256] = jnp.where(low, kv_even, swap(qo_odd)).astype(BF16)
        gp[:, g * 384 + 256 : g * 384 + 384] = rkv[2 * g + 1]
    ag1 = reduce_gather(1, dp1)
    grad_hidden = dot_nt(gp[...], wqkv_ref[...])
    normed = normed_ref[...]
    inner = jnp.mean(grad_hidden * normed, axis=-1, keepdims=True)
    gtok_ref[...] = ((grad_hidden - normed * inner) / spread_ref[...]).astype(BF16)

    for copy in ag0 + ag1:
        copy.wait_recv()
    first = fin[0].reshape(BLK, D).astype(F32)
    second = fin[1].reshape(BLK, D).astype(F32)
    gwo_ref[...] = first[HD : 2 * HD, :]
    rows = jnp.concatenate([first[0:HD, :], second, jnp.zeros((HD, D), F32)], axis=0)
    gqkv_ref[...] = rows.T[:, 0 : 3 * HD]

    for copy in pending:
        copy.wait_send()


def body(tokens, bin_ids, pattern, w_qkv, w_out, head_bias, grad_output):
    vmem = pl.BlockSpec(memory_space=pltpu.VMEM)
    smem = pl.BlockSpec(memory_space=pltpu.SMEM)
    dma = pltpu.SemaphoreType.DMA
    blocks = functools.partial(pltpu.VMEM, dtype=BF16)
    scratch = [
        blocks((NB, BLK, 128)),
        blocks((NB, BLK, 128)),
        blocks((8, BLK, D)),
        blocks((8, BLK, D)),
        blocks((8, BLK, 128)),
        blocks((8, BLK, 128)),
        pltpu.VMEM((BLK, D), F32),
        pltpu.VMEM((BLK, 1), F32),
        blocks((NNZ * BLK, 128)),
        blocks((2 * BLK, 128)),
        pltpu.VMEM((2 * BLK, NNZ * BLK), F32),
        blocks((2 * BLK, NNZ * BLK)),
        pltpu.VMEM((BLK, BLK), F32),
        pltpu.VMEM((BLK, BLK), F32),
        pltpu.VMEM((2 * NB, BLK), F32),
        pltpu.VMEM((NB, BLK), F32),
        pltpu.VMEM((BLK, BLK), F32),
        blocks((8, BLK, 128)),
        blocks((8, BLK, 128)),
        blocks((8, BLK, 128)),
        blocks((8, BLK, 128)),
        blocks((BLK, PER * BLK)),
        blocks((BLK, PER * BLK)),
        pltpu.VMEM((2, BLK, D), F32),
        blocks((2, 8, 16, D)),
        blocks((2, 8, 16, D)),
        blocks((2, 4, 16, D)),
        blocks((2, 8, 16, D)),
        blocks((BLK, D)),
        blocks((BLK, 3 * D)),
        dma((11, 8)),
        dma((11, 8)),
        dma((2, 4)),
        dma((2, 4)),
        dma((2, 2, 5, 2)),
        dma((2, 2, 5, 2)),
    ]
    result, grad_input, own_qkv, own_out = pl.pallas_call(
        kernel,
        out_shape=(
            jax.ShapeDtypeStruct((BLK, D), BF16),
            jax.ShapeDtypeStruct((BLK, D), BF16),
            jax.ShapeDtypeStruct((D, 3 * HD), F32),
            jax.ShapeDtypeStruct((HD, D), F32),
        ),
        in_specs=[smem, smem, vmem, vmem, vmem, vmem, vmem],
        out_specs=(vmem, vmem, vmem, vmem),
        scratch_shapes=scratch,
        compiler_params=pltpu.CompilerParams(
            collective_id=0, has_side_effects=True, vmem_limit_bytes=48 * 1024 * 1024
        ),
        name="layer",
    )(
        pattern[0],
        head_bias,
        tokens[0],
        grad_output[0],
        w_qkv,
        w_out,
        bin_ids[0].reshape(NB, BLK),
    )
    return (result[None], grad_input[None], own_qkv, own_out)


def solution(mesh):
    return jax.shard_map(
        body,
        mesh=mesh,
        in_specs=(
            P("dp", ("seq", "head"), None),
            P("dp", None),
            P("dp", None, None),
            P(),
            P(),
            P(),
            P("dp", ("seq", "head"), None),
        ),
        out_specs=(
            P("dp", ("seq", "head"), None),
            P("dp", ("seq", "head"), None),
            P(None, "head"),
            P("head", None),
        ),
        check_vma=False,
    )
```

time: 560 us -> 105 us (0.19)
  waiting for transfers between devices: 349 us -> 0 us
  Pallas kernels: 0 us -> 94.3 us
  local copies, waits for them, and re-layouts: 90.9 us -> 9.34 us
  other arithmetic: 41.3 us -> 0 us
  matrix products: 35.3 us -> 0 us
  between operations: 14.1 us -> 0.65 us
  starting transfers between devices: 13.3 us -> 0 us
  blocking collectives: 12.8 us -> 0 us
    psum x1 -> x0, waiting for transfers between devices: 262 us -> none  [body(): lax.psum((local_qkv, local_out), ('dp', 'seq', 'head'))]
    pallas_call x0 -> x1, Pallas kernels: none -> 94.3 us  [body(): pl.pallas_call(kernel, out_shape=(jax.ShapeDtypeStruct((BLK, D), BF16), j...]
    reduce_scatter x1 -> x0, waiting for transfers between devices: 47.4 us -> none  [body(): lax.psum_scatter(pair_sums.reshape(seq_length, local_heads, 2 * HD), 'seq...]
    dot_general x20 -> x0, matrix products: 35.3 us -> none  [the longest x4 15.7 us: query_scores(): jnp.einsum('gqhe,gnkhe->ghqnk', query_blk, key_blk, preferred_element_typ...]
    all_gather x1 -> x0, waiting for transfers between devices: 34.8 us -> none  [body(): pair_all = lax.all_gather(pair_local, 'seq', axis=0, tiled=True)]
    gather x16 -> x0, local copies, waits for them, and re-layouts: 20.1 us -> none  [the longest x4 10.2 us: forward_group(): pair_blk = jnp.take(pair_table, key_rows, axis=0)]
    scatter-add x2 -> x0, other arithmetic: 20 us -> none  [scatter_step(): carried = carried.at[key_rows.reshape(-1)].add(both_parts)]
    reshape x11 -> x0, local copies, waits for them, and re-layouts: 14 us -> none  [the longest x4 12.5 us: query_scores(): return scores.reshape(scores.shape[0], scores.shape[1], scores.shape[2], -1)]
  transfers between devices with their start and end apart: 6 -> 0, of which waited for: 4 -> 0; matrix products, arithmetic and copies ran while one was open for 10% -> 0% of each run, Pallas kernels for 0% -> 0%
where the time goes in v1:
time: 105 us; the launch traced here: 104 us
  Pallas kernels  94.3 us (90%)
  local copies, waits for them, and re-layouts  9.34 us (9%)
    pallas_call x1, Pallas kernels, body(): pl.pallas_call(kernel, out_shape=(jax.ShapeDtypeStruct((BLK, D), BF16), j...  94.3 us
    unnamed x17, local copies, waits for them, and re-layouts  9.34 us

profile of v1, /device:TPU:1, one launch (start us, length us, event | category | flops | bytes accessed | tf_op | source)
XLA Modules:
  0.0 104.3 jit_solution(12105746957638023786)
XLA Ops:
  0.6 0.8 copy.11
  1.4 0.0 copy-start
  1.4 1.4 %copy-done = bf16[512,1536]{1,0:T(8,128)(2,1)S(1)} copy-done((bf16[512,1536]{1,0:T(8,128)(2,1)S(1)}, bf16[512,1536]{1,0:T(8,128)(2,1)}, u32[]{:S(2)}) %copy-start) | copy-done | bytes 1572888
  2.8 0.0 copy-start.1
  2.8 1.0 copy-done.1
  3.9 0.0 copy-start.2
  3.9 0.9 copy-done.2
  4.8 0.0 copy-start.3
  4.8 0.9 copy-done.3
  5.7 0.0 copy-start.4
  5.7 0.8 copy-done.4
  6.4 0.0 copy-start.5
  6.4 0.7 copy-done.5
  7.1 94.3 %layer.1 = (bf16[128,512]{1,0:T(8,128)(2,1)S(1)}, bf16[128,512]{1,0:T(8,128)(2,1)S(1)}, f32[512,192]{1,0:T(8,128)S(1)}, f32[64,512]{1,0:T(8,128)S(1)}) custom-call(s32[64,9]{1,0:T(8,128)S(1)} %bitcast.6, f32[8]{0:T(128)S(1)} %copy-done.5, bf16[128,512]{1,0:T(8,128)(2,1)S(1)} %bitcast.9, bf16[128,512]{1,0:T(8,128)(2,1)S(1)} %bitcast.10, ...), custom_call_target="tpu_custom_call" | custom-call | tf_op jit(solution)/shard_map/layer/pallas_call | solution.py:396
  101.4 0.9 copy.12
  102.3 0.7 copy.16
  102.9 0.7 copy.17
  103.6 0.7 copy.18
Async XLA Ops:
  1.4 1.4 %copy-start = (bf16[512,1536]{1,0:T(8,128)(2,1)S(1)}, bf16[512,1536]{1,0:T(8,128)(2,1)}, u32[]{:S(2)}) copy-start(bf16[512,1536]{1,0:T(8,128)(2,1)} %wqkv_ref.1) | copy-start | bytes 4718596
  2.8 1.0 copy-start.1
  3.9 0.9 copy-start.2
  4.8 0.9 copy-start.3
  5.7 0.8 copy-start.4
  6.4 0.7 copy-start.5

commit v2 on v1

v2 whole, which is shorter than its diff:
```python
import functools
import math

import jax
import jax.numpy as jnp
from jax import lax
from jax.experimental import pallas as pl
from jax.experimental.pallas import tpu as pltpu
from jax.sharding import PartitionSpec as P

D = 512
HEADS = 8
HD = 64
BLK = 128
NNZ = 9
PER = 8
NB = 64
EPSILON = 1e-05
LOG2E = math.log2(math.e)
MESH = pl.DeviceIdType.MESH
F32 = jnp.float32
BF16 = jnp.bfloat16
CAT = NNZ * BLK

BATCHES = ((0, 1), (1, 2), (3, 2), (5, 2), (7, 1))

(
    Z_BQO, Z_BKV, Z_S3A, Z_S3B, G_ST, G_S1A, G_S1B, G_S4A, G_S4B,
) = range(9)


def dot_nn(a, b):
    return lax.dot_general(a, b, (((1,), (0,)), ((), ())), preferred_element_type=F32)


def dot_nt(a, b):
    return lax.dot_general(a, b, (((1,), (1,)), ((), ())), preferred_element_type=F32)


def place(rel):
    return jnp.where(rel == 0, 0, jnp.where(rel <= 4, 2 * rel - 1, 16 - 2 * rel))


def tile(n):
    return slice(n * BLK, (n + 1) * BLK)


def kernel(
    bias_ref, tok_hbm, gout_hbm, wqkv_hbm, wout_hbm, aux_hbm,
    out_hbm, gtok_hbm, gqkv_ref, gwo_ref,
    gkv, gqd, hid, gog, tok, wqkv, wout, aux, pat, wcat, wo2, normed_ref, spread_ref,
    ycats, ycat, probs, sd, pd, a2, stcol, strow, stg, deltas, invs, binsf, binst,
    obuf, bqo, bkv, rqo, rkv, dtqo, dtkv,
    wpart, ars, arr, dpx, zbc, fin, att, gp, res, gres,
    ss, rr, ys, yr, zs, zr, xs, xr, ins, sws, swr,
):
    dp = lax.axis_index("dp")
    z = lax.axis_index("seq")
    head = lax.axis_index("head")
    yhi, c = dp // 2, lax.rem(dp, 2)
    x, ylo = head // 2, lax.rem(head, 2)
    r = 2 * x + c
    seqno = 2 * yhi + ylo
    moved = c != ylo
    odd = lax.rem(z, 2) == 1
    factor = 1.0 / math.sqrt(HD)
    c2 = factor * LOG2E

    def mod8(v):
        return lax.rem(v + 16, 8)

    def device(xx, cc):
        return {"dp": 2 * yhi + cc, "head": 2 * xx + ylo}

    partner = {"dp": 2 * yhi + ylo, "head": 2 * x + c}
    sibling = {"dp": 2 * yhi + (1 - c)}

    def member(d):
        dx, dc = d // 2, d % 2
        xx = lax.rem(x + dx, 4)
        cc = c if dc == 0 else 1 - c
        return xx, cc

    def giver(d):
        dx, dc = d // 2, d % 2
        xx = lax.rem(x + 4 - dx, 4)
        cc = c if dc == 0 else 1 - c
        return 2 * xx + cc

    def remote(src, dst, ssem, rsem, dev):
        return pltpu.make_async_remote_copy(
            src_ref=src, dst_ref=dst, send_sem=ssem, recv_sem=rsem,
            device_id=dev, device_id_type=MESH,
        )

    pending = []

    def start(copy):
        copy.start()
        pending.append(copy)
        return copy

    def when(cond, fn):
        pl.when(cond)(fn)

    barrier = pltpu.get_barrier_semaphore()

    def greet(dev):
        pl.semaphore_signal(barrier, inc=1, device_id=dev, device_id_type=MESH)

    for d in range(1, 8):
        greet({"seq": mod8(z + d)})
        greet(device(*member(d)))
    others = []
    for e in range(1, 4):
        yh = yhi if e // 2 == 0 else 1 - yhi
        yl = ylo if e % 2 == 0 else 1 - ylo
        others.append({"dp": 2 * yh + c, "head": 2 * x + yl})
        greet(others[-1])
    when(moved, lambda: greet(partner))

    weights = [
        pltpu.make_async_copy(wqkv_hbm, wqkv, ins.at[0]),
        pltpu.make_async_copy(wout_hbm, wout, ins.at[1]),
    ]
    stay = [
        pltpu.make_async_copy(tok_hbm, tok, ins.at[2]),
        pltpu.make_async_copy(gout_hbm, gog.at[0], ins.at[3]),
        pltpu.make_async_copy(aux_hbm, aux, ins.at[4]),
    ]
    go = [
        remote(tok_hbm, tok, sws.at[0], swr.at[0], partner),
        remote(gout_hbm, gog.at[0], sws.at[1], swr.at[1], partner),
    ]
    share = remote(aux_hbm, aux, sws.at[2], swr.at[2], sibling)
    for copy in weights:
        copy.start()
    when(jnp.logical_not(moved), lambda: [copy.start() for copy in stay] and None)

    lane = lax.broadcasted_iota(jnp.int32, (BLK, 2 * HD), 1)
    low = lane < HD

    def swap(v):
        return pltpu.roll(v, HD, 1)

    for copy in weights:
        copy.wait()
    pair = pl.multiple_of((z // 2) * 384, 128)
    for q in range(4):
        rows = slice(128 * q, 128 * (q + 1))
        w0 = wqkv[rows, pl.ds(pair, 128)].astype(F32)
        w1 = wqkv[rows, pl.ds(pair + 128, 128)].astype(F32)
        w2 = wqkv[rows, pl.ds(pair + 256, 128)].astype(F32)
        s1 = swap(w1)
        wcat[rows, 0:128] = jnp.where(odd, w2, jnp.where(low, swap(w0), s1)).astype(BF16)
        wcat[rows, 128:256] = jnp.where(low, jnp.where(odd, s1, w0), 0.0).astype(BF16)
    wo_pair = wout[pl.ds(pl.multiple_of((z // 2) * 128, 128), 128), :]
    wo2[0:HD, :] = jnp.zeros((HD, D), BF16)
    wo2[HD:BLK, :] = jnp.where(odd, wo_pair[HD:BLK, :], wo_pair[0:HD, :])

    pl.semaphore_wait(barrier, 17 + jnp.where(moved, 1, 0))
    when(moved, lambda: [copy.start() for copy in go] and None)
    when(jnp.logical_not(moved), lambda: share.start())

    when(moved, lambda: go[0].wait_recv())
    when(jnp.logical_not(moved), lambda: stay[0].wait())

    tokens = tok[...].astype(F32)
    spread = jnp.sqrt(jnp.mean(tokens * tokens, axis=-1, keepdims=True) + EPSILON)
    normed = tokens / spread
    normed_ref[...] = normed
    spread_ref[...] = spread
    hid[0] = normed.astype(BF16)

    rings = (hid, gog)
    table = {}

    def hop(k, way, t, part):
        if way == 0:
            src, dst = (0 if t == 1 else 2 * (t - 1)), (2 * t if t < 4 else 7)
        else:
            src, dst = (0 if t == 1 else 2 * (t - 1) - 1), 2 * t - 1
        rows = pl.ds(64 * part, 64)
        return remote(
            rings[k].at[src, rows], rings[k].at[dst, rows],
            zs.at[k, way, t, part], zr.at[k, way, t, part],
            {"seq": mod8(z + 1) if way == 0 else mod8(z - 1)},
        )

    def first_hop(k):
        for part in (0, 1):
            for way in (0, 1):
                table[k, way, 1, part] = start(hop(k, way, 1, part))

    def next_hop(k, t):
        for part in (0, 1):
            for way in (0, 1):
                table[k, way, t, part].wait_recv()
                if t + 1 < 4 or (t + 1 == 4 and part == way):
                    table[k, way, t + 1, part] = start(hop(k, way, t + 1, part))

    def last_hop(k):
        for way in (0, 1):
            table[k, way, 4, way].wait_recv()

    pools = (gkv, gqd)
    ring_x = {}
    x_right, x_left = lax.rem(x + 1, 4), lax.rem(x + 3, 4)
    x_far = lax.rem(x + 2, 4)

    def xcopy(k, b, kind, owner, dev):
        first, count = BATCHES[b]
        part = pools[k].at[owner, pl.ds(first, count)]
        ring_x[k, b, kind] = start(
            remote(part, part, xs.at[k, b, kind], xr.at[k, b, kind], dev)
        )

    def x_own(k, b):
        xcopy(k, b, 0, r, device(x_right, c))
        xcopy(k, b, 1, r, device(x_left, c))
        xcopy(k, b, 2, r, sibling)

    def x_pass(k, b):
        ring_x[k, b, 0].wait_recv()
        if b in (0, 1, 4):
            xcopy(k, b, 5, 2 * x_left + c, device(x_right, c))
        xcopy(k, b, 3, 2 * x_left + c, sibling)
        ring_x[k, b, 1].wait_recv()
        if b in (2, 3):
            xcopy(k, b, 5, 2 * x_right + c, device(x_left, c))
        xcopy(k, b, 4, 2 * x_right + c, sibling)

    def x_far_pass(k, b):
        ring_x[k, b, 5].wait_recv()
        xcopy(k, b, 6, 2 * x_far + c, sibling)

    def x_end(k):
        for b in range(5):
            for kind in (2, 3, 4, 6):
                ring_x[k, b, kind].wait_recv()

    def project(b):
        first, count = BATCHES[b]
        for p in range(first, first + count):
            t = dot_nn(hid[p], wcat[...]).astype(BF16)
            gkv[r, p] = t[:, 0:128]
            gqd[r, p] = t[:, 128:256]
        x_own(0, b)

    def project_grad(b):
        first, count = BATCHES[b]
        for p in range(first, first + count):
            u = dot_nt(gog[p], wo2[...])
            gqd[r, p] = jnp.where(low, gqd[r, p], u.astype(BF16))
        x_own(1, b)

    first_hop(0)
    project(0)
    when(moved, lambda: go[1].wait_recv())
    when(jnp.logical_not(moved), lambda: stay[1].wait())
    next_hop(0, 1)
    first_hop(1)
    project(1)
    project_grad(0)
    x_pass(0, 0)
    next_hop(0, 2)
    project(2)
    x_pass(0, 1)
    x_far_pass(0, 0)
    next_hop(1, 1)
    project_grad(1)
    next_hop(0, 3)
    project(3)
    x_pass(0, 2)
    x_far_pass(0, 1)
    x_pass(1, 0)
    next_hop(1, 2)
    project_grad(2)
    last_hop(0)
    project(4)
    x_pass(0, 3)
    x_far_pass(0, 2)
    x_pass(1, 1)
    x_far_pass(1, 0)

    when(moved, lambda: share.wait_recv())
    when(jnp.logical_not(moved), lambda: stay[2].wait())
    to_scalars = pltpu.make_async_copy(aux.at[pl.ds(NB, 8)], pat, ins.at[5])
    to_scalars.start()
    binsf[...] = aux[0:NB, :].astype(F32)
    binst[...] = jnp.concatenate([binsf[...], jnp.zeros((BLK - NB, BLK), F32)], axis=0).T
    to_scalars.wait()

    x_pass(0, 4)
    x_far_pass(0, 3)
    next_hop(1, 3)
    project_grad(3)
    x_far_pass(0, 4)
    x_pass(1, 2)
    x_far_pass(1, 1)
    x_end(0)

    bias2 = bias_ref[z] * LOG2E

    def own_block(p):
        t = (p + 1) // 2
        rel = jnp.where(lax.rem(p, 2) == 1, t, -t)
        return 8 * mod8(z + rel) + r

    def used_block(row, n):
        other = lax.rem(row + pat[0, n], NB)
        return other, lax.rem(other, 8), place(mod8(other // 8 - z))

    def own_bins(row):
        return jnp.sum(jnp.where(lane == row, binst[...], 0.0), axis=1, keepdims=True)

    stcol[...] = jnp.zeros((BLK, BLK), F32)

    def forward_block(p, carry):
        row = own_block(p)
        for n in range(NNZ):
            _, rn, pn = used_block(row, n)
            ycats[p, tile(n), :] = gkv[rn, pn]
        query = gqd[r, p]
        sd[0:BLK, :] = dot_nt(jnp.where(low, query, jnp.zeros_like(query)), ycats[p])
        bin_col = own_bins(row)
        top = None
        for n in range(NNZ):
            other, _, _ = used_block(row, n)
            bin_row = binsf[pl.ds(other, 1), :]
            v = sd[0:BLK, tile(n)] * c2 + jnp.where(bin_col == bin_row, bias2, 0.0)
            sd[0:BLK, tile(n)] = v
            top = v if top is None else jnp.maximum(top, v)
        m = jnp.max(top, axis=1, keepdims=True)
        total = jnp.zeros((BLK, BLK), F32)
        for n in range(NNZ):
            e = jnp.exp2(sd[0:BLK, tile(n)] - m)
            probs[p, :, tile(n)] = e
            pd[0:BLK, tile(n)] = e.astype(BF16)
            total = total + e
        total = jnp.sum(total, axis=1, keepdims=True)
        inv = 1.0 / total
        obuf[p] = (dot_nn(pd[0:BLK, :], ycats[p]) * inv).astype(BF16)
        invs[p] = inv
        stcol[...] = jnp.where(lane == 2 * p, m + jnp.log2(total), stcol[...])
        return carry

    lax.fori_loop(0, PER, forward_block, 0)

    x_pass(1, 3)
    x_far_pass(1, 2)
    last_hop(1)
    project_grad(4)

    for p in range(PER):
        both = gqd[r, p].astype(F32) * obuf[p].astype(F32)
        delta = jnp.sum(jnp.where(low, 0.0, both), axis=1, keepdims=True)
        deltas[p] = delta
        stcol[...] = jnp.where(lane == 2 * p + 1, delta, stcol[...])
    strow[...] = stcol[...].T
    mine = stg.at[pl.ds(pl.multiple_of(2 * PER * r, 16), 16)]
    stg[pl.ds(pl.multiple_of(2 * PER * r, 16), 16), :] = strow[0:16, :]

    def group(kind, d, src, dst):
        return start(remote(src, dst, ss.at[kind, d], rr.at[kind, d], device(*member(d))))

    def along(kind, d, src, dst):
        return start(remote(src, dst, ss.at[kind, d], rr.at[kind, d], {"seq": mod8(z + d)}))

    c_st = [group(G_ST, d, mine, mine) for d in range(1, 8)]
    x_pass(1, 4)
    x_far_pass(1, 3)

    def query_block(p, carry):
        block = gqd[r, p]
        sd[0:BLK, :] = dot_nt(jnp.where(low, jnp.zeros_like(block), block), ycats[p])
        delta = deltas[p]
        for n in range(NNZ):
            pd[0:BLK, tile(n)] = (
                probs[p, :, tile(n)] * (sd[0:BLK, tile(n)] - delta)
            ).astype(BF16)
        grad = dot_nn(pd[0:BLK, :], ycats[p]) * (invs[p] * factor)
        both = jnp.where(low, grad, obuf[p].astype(F32))
        bqo[p] = both.astype(BF16)
        dtqo[:, pl.ds(pl.multiple_of(p * BLK, BLK), BLK)] = both.T.astype(BF16)
        return carry

    lax.fori_loop(0, PER, query_block, 0)

    far = (0, 1, 3, 5, 7, 6, 4, 2)
    rqo[z] = bqo[0]
    c_bqo = [along(Z_BQO, d, bqo.at[far[d]], rqo.at[z]) for d in range(1, 8)]
    x_far_pass(1, 4)

    def stage1(k, part):
        wpart[k] = part
        for q in range(8):
            ars[k, q] = part[16 * q : 16 * (q + 1), :].astype(BF16)
        sent = []
        for d in range(1, 8):
            xx, cc = member(d)
            sent.append(group((G_S1A, G_S1B)[k], d, ars.at[k, 2 * xx + cc], arr.at[k, r]))
        return sent

    def stage2(k, copies):
        total = wpart[k, pl.ds(pl.multiple_of(16 * r, 16), 16), :]
        for d, copy in zip(range(1, 8), copies):
            copy.wait_recv()
            total = total + arr[k, giver(d)].astype(F32)
        dpx[k, seqno] = total.astype(BF16)
        slot = dpx.at[k, seqno]
        return [
            start(remote(slot, slot, ys.at[k, e], yr.at[k, e], others[e - 1]))
            for e in range(1, 4)
        ]

    mine_here = lax.rem(z, 2) == ylo

    def stage3(k, copies):
        for copy in copies:
            copy.wait_recv()
        total = dpx[k, 0].astype(F32)
        for q in range(1, 4):
            total = total + dpx[k, q].astype(F32)

        def spread_out():
            zbc[k, z // 2] = total.astype(BF16)

        slot = zbc.at[k, z // 2]
        kind = (Z_S3A, Z_S3B)[k]
        sent = [
            remote(slot, slot, ss.at[kind, d], rr.at[kind, d], {"seq": mod8(z + d)})
            for d in range(1, 8)
        ]
        when(mine_here, spread_out)
        when(mine_here, lambda: [copy.start() for copy in sent] and None)
        return sent

    def stage4(k, copies):
        for d, copy in zip(range(1, 8), copies):
            when(lax.rem(z + 8 - d, 2) == ylo, lambda: copy.wait_recv())
        fin[k, r] = zbc[k, x]
        sent = []
        for d in range(1, 8):
            xx, _ = member(d)
            sent.append(group((G_S4A, G_S4B)[k], d, zbc.at[k, xx], fin.at[k, r]))
        when(mine_here, lambda: [copy.wait_send() for copy in copies] and None)
        return sent

    hid_all = hid[...].reshape(PER * BLK, D)
    go_all = gog[...].reshape(PER * BLK, D)
    part0 = jnp.concatenate(
        [dot_nn(dtqo[0:HD, :], hid_all), dot_nn(dtqo[HD : 2 * HD, :], go_all)], axis=0
    )
    s1a = stage1(0, part0)
    for copy in c_st:
        copy.wait_recv()
    x_end(1)

    def key_block(p, carry):
        row = own_block(p)
        for n in range(NNZ):
            _, rn, pn = used_block(row, n)
            ycat[tile(n), :] = gqd[rn, pn]
        block = gkv[r, p]
        zero = jnp.zeros_like(block)
        a2[0:BLK, :] = jnp.where(low, block, zero)
        a2[BLK : 2 * BLK, :] = jnp.where(low, zero, block)
        sd[...] = dot_nt(a2[...], ycat[...])
        bin_col = own_bins(row)
        for n in range(NNZ):
            other, rn, pn = used_block(row, n)
            bin_row = binsf[pl.ds(other, 1), :]
            log_row = stg[pl.ds(16 * rn + 2 * pn, 1), :]
            delta_row = stg[pl.ds(16 * rn + 2 * pn + 1, 1), :]
            v = sd[0:BLK, tile(n)] * c2 + jnp.where(bin_col == bin_row, bias2, 0.0)
            e = jnp.exp2(v - log_row)
            pd[0:BLK, tile(n)] = e.astype(BF16)
            pd[BLK : 2 * BLK, tile(n)] = (e * (sd[BLK : 2 * BLK, tile(n)] - delta_row)).astype(BF16)
        g = dot_nn(pd[...], ycat[...])
        both = jnp.where(low, g[BLK : 2 * BLK] * factor, g[0:BLK])
        bkv[p] = both.astype(BF16)
        dtkv[:, pl.ds(pl.multiple_of(p * BLK, BLK), BLK)] = both.T.astype(BF16)
        return carry

    lax.fori_loop(0, PER, key_block, 0)

    rkv[z] = bkv[0]
    c_bkv = [along(Z_BKV, d, bkv.at[far[d]], rkv.at[z]) for d in range(1, 8)]
    s1b = stage1(1, dot_nn(dtkv[...], hid[...].reshape(PER * BLK, D)))
    s2a = stage2(0, s1a)

    def deliver(src, dst, k):
        here = pltpu.make_async_copy(src, dst, ins.at[6 + k])
        there = remote(src, dst, sws.at[3 + k], swr.at[3 + k], partner)
        when(jnp.logical_not(moved), lambda: here.start())
        when(moved, lambda: there.start())
        return here, there

    for copy in c_bqo:
        copy.wait_recv()
    for g in range(HEADS // 2):
        even, uneven = rqo[2 * g].astype(F32), rqo[2 * g + 1].astype(F32)
        att[:, tile(g)] = jnp.where(low, swap(even), uneven).astype(BF16)
    res[...] = dot_nn(att[...], wout[...]).astype(BF16)
    d_out = deliver(res, out_hbm, 0)
    s3a = stage3(0, s2a)
    s2b = stage2(1, s1b)
    s4a = stage4(0, s3a)
    s3b = stage3(1, s2b)

    for copy in c_bkv:
        copy.wait_recv()
    for g in range(HEADS // 2):
        qo_even, qo_odd = rqo[2 * g].astype(F32), rqo[2 * g + 1].astype(F32)
        kv_even = swap(rkv[2 * g].astype(F32))
        gp[:, tile(3 * g)] = jnp.where(low, qo_even, kv_even).astype(BF16)
        gp[:, tile(3 * g + 1)] = jnp.where(low, kv_even, swap(qo_odd)).astype(BF16)
        gp[:, tile(3 * g + 2)] = rkv[2 * g + 1]
    grad_hidden = dot_nt(gp[...], wqkv[...])
    s4b = stage4(1, s3b)
    normed = normed_ref[...]
    inner = jnp.mean(grad_hidden * normed, axis=-1, keepdims=True)
    gres[...] = ((grad_hidden - normed * inner) / spread_ref[...]).astype(BF16)
    d_gtok = deliver(gres, gtok_hbm, 1)

    for copy in s4a + s4b:
        copy.wait_recv()
    first = fin[0].reshape(BLK, D).astype(F32)
    second = fin[1].reshape(BLK, D).astype(F32)
    gwo_ref[...] = first[HD : 2 * HD, :]
    rows = jnp.concatenate([first[0:HD, :], second, jnp.zeros((HD, D), F32)], axis=0)
    gqkv_ref[...] = rows.T[:, 0 : 3 * HD]

    for copy in pending:
        copy.wait_send()
    when(moved, lambda: [copy.wait_send() for copy in go] and None)
    when(jnp.logical_not(moved), lambda: share.wait_send())
    for here, there in (d_out, d_gtok):
        when(jnp.logical_not(moved), lambda: here.wait())
        when(moved, lambda: there.wait())


def body(tokens, bin_ids, pattern, w_qkv, w_out, head_bias, grad_output):
    vmem = pl.BlockSpec(memory_space=pltpu.VMEM)
    smem = pl.BlockSpec(memory_space=pltpu.SMEM)
    hbm = pl.BlockSpec(memory_space=pltpu.HBM)
    dma = pltpu.SemaphoreType.DMA
    half = functools.partial(pltpu.VMEM, dtype=BF16)
    full = functools.partial(pltpu.VMEM, dtype=F32)
    scratch = [
        half((8, 8, BLK, 128)),
        half((8, 8, BLK, 128)),
        half((8, BLK, D)),
        half((8, BLK, D)),
        half((BLK, D)),
        half((D, 3 * D)),
        half((D, D)),
        pltpu.VMEM((NB + 8, BLK), jnp.int32),
        pltpu.SMEM((8, BLK), jnp.int32),
        half((D, 256)),
        half((BLK, D)),
        full((BLK, D)),
        full((BLK, 1)),
        half((PER, CAT, 128)),
        half((CAT, 128)),
        full((PER, BLK, CAT)),
        full((2 * BLK, CAT)),
        half((2 * BLK, CAT)),
        half((2 * BLK, 128)),
        full((BLK, BLK)),
        full((BLK, BLK)),
        full((2 * NB, BLK)),
        full((PER, BLK, 1)),
        full((PER, BLK, 1)),
        full((NB, BLK)),
        full((BLK, BLK)),
        half((8, BLK, 128)),
        half((8, BLK, 128)),
        half((8, BLK, 128)),
        half((8, BLK, 128)),
        half((8, BLK, 128)),
        half((BLK, PER * BLK)),
        half((BLK, PER * BLK)),
        full((2, BLK, D)),
        half((2, 8, 16, D)),
        half((2, 8, 16, D)),
        half((2, 4, 16, D)),
        half((2, 4, 16, D)),
        half((2, 8, 16, D)),
        half((BLK, D)),
        half((BLK, 3 * D)),
        half((BLK, D)),
        half((BLK, D)),
        dma((9, 8)),
        dma((9, 8)),
        dma((2, 4)),
        dma((2, 4)),
        dma((2, 2, 5, 2)),
        dma((2, 2, 5, 2)),
        dma((2, 5, 7)),
        dma((2, 5, 7)),
        dma((8,)),
        dma((5,)),
        dma((5,)),
    ]
    aux = jnp.concatenate(
        [bin_ids[0].reshape(NB, BLK), jnp.pad(pattern[0, 0:1], ((0, 7), (0, BLK - NNZ)))], axis=0
    )
    result, grad_input, own_qkv, own_out = pl.pallas_call(
        kernel,
        out_shape=(
            jax.ShapeDtypeStruct((BLK, D), BF16),
            jax.ShapeDtypeStruct((BLK, D), BF16),
            jax.ShapeDtypeStruct((D, 3 * HD), F32),
            jax.ShapeDtypeStruct((HD, D), F32),
        ),
        in_specs=[smem, hbm, hbm, hbm, hbm, hbm],
        out_specs=(hbm, hbm, vmem, vmem),
        scratch_shapes=scratch,
        compiler_params=pltpu.CompilerParams(
            collective_id=0, has_side_effects=True, vmem_limit_bytes=48 * 1024 * 1024
        ),
        name="layer",
    )(head_bias, tokens[0], grad_output[0], w_qkv, w_out, aux)
    return (result[None], grad_input[None], own_qkv, own_out)


def solution(mesh):
    return jax.shard_map(
        body,
        mesh=mesh,
        in_specs=(
            P("dp", ("seq", "head"), None),
            P("dp", None),
            P("dp", None, None),
            P(),
            P(),
            P(),
            P("dp", ("seq", "head"), None),
        ),
        out_specs=(
            P("dp", ("seq", "head"), None),
            P("dp", ("seq", "head"), None),
            P(None, "head"),
            P("head", None),
        ),
        check_vma=False,
    )
```

time: 105 us -> 93.5 us (0.89)
  Pallas kernels: 94.3 us -> 83.1 us
    pallas_call x1, Pallas kernels: 94.3 us -> 83.1 us  [body(): pl.pallas_call(kernel, out_shape=(jax.ShapeDtypeStruct((BLK, D), BF16), j...]
    unnamed x17 -> x14, local copies, waits for them, and re-layouts: 9.34 us -> 7.81 us
where the time goes in v2:
time: 93.5 us; the launch traced here: 93.2 us
  Pallas kernels  83.1 us (89%)
  local copies, waits for them, and re-layouts  8.76 us (9%)
    pallas_call x1, Pallas kernels, body(): pl.pallas_call(kernel, out_shape=(jax.ShapeDtypeStruct((BLK, D), BF16), j...  83.1 us
    unnamed x14, local copies, waits for them, and re-layouts  7.81 us

profile of v2, /device:TPU:1, one launch (start us, length us, event | category | flops | bytes accessed | tf_op | source)
XLA Modules:
  0.0 93.2 jit_solution(9257071438676699894)
XLA Ops:
  0.6 1.0 %slice_reduce_fusion = s32[9]{0:T(128)S(1)} fusion(s32[1,64,9]{1,0,2:T(1,128)} %param.9), kind=kLoop, calls=%fused_computation.1 | loop fusion | bytes 72 | tf_op jit(solution)/shard_map/slice | solution.py:608
  1.6 0.8 pad_add_fusion.aux_hbm
  2.4 0.0 copy-start
  2.4 1.4 %copy-done = bf16[512,1536]{1,0:T(8,128)(2,1)S(1)} copy-done((bf16[512,1536]{1,0:T(8,128)(2,1)S(1)}, bf16[512,1536]{1,0:T(8,128)(2,1)}, u32[]{:S(2)}) %copy-start) | copy-done | bytes 1572888
  3.8 0.0 copy-start.1
  3.8 1.0 %copy-done.1 = bf16[512,512]{1,0:T(8,128)(2,1)S(1)} copy-done((bf16[512,512]{1,0:T(8,128)(2,1)S(1)}, bf16[512,512]{1,0:T(8,128)(2,1)}, u32[]{:S(2)}) %copy-start.1) | copy-done | bytes 524312
  4.8 0.0 copy-start.2
  4.8 0.9 copy-done.2
  5.7 0.0 copy-start.3
  5.7 0.9 copy-done.3
  6.6 0.0 copy-start.4
  6.6 0.7 copy-done.4
  7.3 83.1 %layer.1 = (bf16[128,512]{1,0:T(8,128)(2,1)S(1)}, bf16[128,512]{1,0:T(8,128)(2,1)S(1)}, f32[512,192]{1,0:T(8,128)S(1)}, f32[64,512]{1,0:T(8,128)S(1)}) custom-call(f32[8]{0:T(128)S(1)} %copy-done.4, bf16[128,512]{1,0:T(8,128)(2,1)S(1)} %bitcast.8, bf16[128,512]{1,0:T(8,128)(2,1)S(1)} %bitcast.9, bf16[512,1536]{1,0:T(8,128)(2,1)S(1)} %copy-done, ...), custom_call_target="tpu_custom_call" | custom-call | tf_op jit(solution)/shard_map/layer/pallas_call | solution.py:610
  90.3 0.9 copy.12
  91.3 0.7 copy.16
  91.9 0.7 copy.17
  92.6 0.7 copy.18
Async XLA Ops:
  2.4 1.4 %copy-start = (bf16[512,1536]{1,0:T(8,128)(2,1)S(1)}, bf16[512,1536]{1,0:T(8,128)(2,1)}, u32[]{:S(2)}) copy-start(bf16[512,1536]{1,0:T(8,128)(2,1)} %wqkv_hbm.1) | copy-start | bytes 4718596
  3.8 1.0 %copy-start.1 = (bf16[512,512]{1,0:T(8,128)(2,1)S(1)}, bf16[512,512]{1,0:T(8,128)(2,1)}, u32[]{:S(2)}) copy-start(bf16[512,512]{1,0:T(8,128)(2,1)} %wout_hbm.1) | copy-start | bytes 1572868
  4.8 0.9 copy-start.2
  5.7 0.9 copy-start.3
  6.6 0.7 copy-start.4

commit v3 on v2

--- a/solution.py
+++ b/solution.py
@@ -46,12 +46,12 @@
 
 
 def kernel(
-    bias_ref, tok_hbm, gout_hbm, wqkv_hbm, wout_hbm, aux_hbm,
-    out_hbm, gtok_hbm, gqkv_ref, gwo_ref,
-    gkv, gqd, hid, gog, tok, wqkv, wout, aux, pat, wcat, wo2, normed_ref, spread_ref,
+    bias_ref, tok_hbm, gout_hbm, wqkv_hbm, wout_hbm, bins_hbm, pat_hbm,
+    out_hbm, gtok_hbm, fin,
+    gkv, gqd, hid, gog, tok, wqkv, wout, bins, patv, pat, wcat, wo2, normed_ref, spread_ref,
     ycats, ycat, probs, sd, pd, a2, stcol, strow, stg, deltas, invs, binsf, binst,
     obuf, bqo, bkv, rqo, rkv, dtqo, dtkv,
-    wpart, ars, arr, dpx, zbc, fin, att, gp, res, gres,
+    wpart, ars, arr, dpx, zbc, att, gp, res, gres,
     ss, rr, ys, yr, zs, zr, xs, xr, ins, sws, swr,
 ):
     dp = lax.axis_index("dp")
@@ -126,13 +126,17 @@
     stay = [
         pltpu.make_async_copy(tok_hbm, tok, ins.at[2]),
         pltpu.make_async_copy(gout_hbm, gog.at[0], ins.at[3]),
-        pltpu.make_async_copy(aux_hbm, aux, ins.at[4]),
+        pltpu.make_async_copy(bins_hbm, bins, ins.at[4]),
+        pltpu.make_async_copy(pat_hbm, patv, ins.at[5]),
     ]
     go = [
         remote(tok_hbm, tok, sws.at[0], swr.at[0], partner),
         remote(gout_hbm, gog.at[0], sws.at[1], swr.at[1], partner),
     ]
-    share = remote(aux_hbm, aux, sws.at[2], swr.at[2], sibling)
+    share = [
+        remote(bins_hbm, bins, sws.at[2], swr.at[2], sibling),
+        remote(pat_hbm, patv, sws.at[5], swr.at[5], sibling),
+    ]
     for copy in weights:
         copy.start()
     when(jnp.logical_not(moved), lambda: [copy.start() for copy in stay] and None)
@@ -160,7 +164,7 @@
 
     pl.semaphore_wait(barrier, 17 + jnp.where(moved, 1, 0))
     when(moved, lambda: [copy.start() for copy in go] and None)
-    when(jnp.logical_not(moved), lambda: share.start())
+    when(jnp.logical_not(moved), lambda: [copy.start() for copy in share] and None)
 
     when(moved, lambda: go[0].wait_recv())
     when(jnp.logical_not(moved), lambda: stay[0].wait())
@@ -262,53 +266,67 @@
     first_hop(1)
     project(1)
     project_grad(0)
-    x_pass(0, 0)
     next_hop(0, 2)
     project(2)
+    x_pass(0, 0)
     x_pass(0, 1)
-    x_far_pass(0, 0)
     next_hop(1, 1)
     project_grad(1)
     next_hop(0, 3)
     project(3)
+    x_far_pass(0, 0)
     x_pass(0, 2)
-    x_far_pass(0, 1)
     x_pass(1, 0)
+    last_hop(0)
+    project(4)
     next_hop(1, 2)
     project_grad(2)
-    last_hop(0)
-    project(4)
+    x_far_pass(0, 1)
     x_pass(0, 3)
     x_far_pass(0, 2)
+    x_pass(0, 4)
     x_pass(1, 1)
-    x_far_pass(1, 0)
-
-    when(moved, lambda: share.wait_recv())
-    when(jnp.logical_not(moved), lambda: stay[2].wait())
-    to_scalars = pltpu.make_async_copy(aux.at[pl.ds(NB, 8)], pat, ins.at[5])
+
+    when(moved, lambda: [copy.wait_recv() for copy in share] and None)
+    when(jnp.logical_not(moved), lambda: [copy.wait() for copy in stay[2:]] and None)
+    to_scalars = pltpu.make_async_copy(patv, pat, ins.at[8])
     to_scalars.start()
-    binsf[...] = aux[0:NB, :].astype(F32)
+    for q in range(NB):
+        binsf[q : q + 1, :] = bins[:, tile(q)].astype(F32)
     binst[...] = jnp.concatenate([binsf[...], jnp.zeros((BLK - NB, BLK), F32)], axis=0).T
     to_scalars.wait()
 
-    x_pass(0, 4)
     x_far_pass(0, 3)
+    x_far_pass(0, 4)
     next_hop(1, 3)
     project_grad(3)
-    x_far_pass(0, 4)
-    x_pass(1, 2)
-    x_far_pass(1, 1)
     x_end(0)
 
     bias2 = bias_ref[z] * LOG2E
 
+    def distance(p):
+        t = (p + 1) // 2
+        return jnp.where(lax.rem(p, 2) == 1, t, 8 - t)
+
     def own_block(p):
-        t = (p + 1) // 2
-        rel = jnp.where(lax.rem(p, 2) == 1, t, -t)
-        return 8 * mod8(z + rel) + r
+        return 8 * mod8(z + distance(p)) + r
+
+    far = (0, 1, 3, 5, 7, 6, 4, 2)
+
+    def back(kind, src, dst, d):
+        return remote(src, dst, ss.at[kind, d], rr.at[kind, d], {"seq": mod8(z + d)})
+
+    def leave(kind, buf, dst, p):
+        when(p > 0, lambda: back(kind, buf.at[p], dst.at[z], distance(p)).start())
+
+    def left(kind, buf, dst):
+        dst[z] = buf[0]
+        copies = [back(kind, buf.at[far[d]], dst.at[z], d) for d in range(1, 8)]
+        pending.extend(copies)
+        return copies
 
     def used_block(row, n):
-        other = lax.rem(row + pat[0, n], NB)
+        other = lax.rem(row + pat[n, 0, 0], NB)
         return other, lax.rem(other, 8), place(mod8(other // 8 - z))
 
     def own_bins(row):
@@ -347,8 +365,6 @@
 
     lax.fori_loop(0, PER, forward_block, 0)
 
-    x_pass(1, 3)
-    x_far_pass(1, 2)
     last_hop(1)
     project_grad(4)
 
@@ -364,12 +380,12 @@
     def group(kind, d, src, dst):
         return start(remote(src, dst, ss.at[kind, d], rr.at[kind, d], device(*member(d))))
 
-    def along(kind, d, src, dst):
-        return start(remote(src, dst, ss.at[kind, d], rr.at[kind, d], {"seq": mod8(z + d)}))
-
     c_st = [group(G_ST, d, mine, mine) for d in range(1, 8)]
+    x_far_pass(1, 0)
+    x_far_pass(1, 1)
+    x_pass(1, 2)
+    x_pass(1, 3)
     x_pass(1, 4)
-    x_far_pass(1, 3)
 
     def query_block(p, carry):
         block = gqd[r, p]
@@ -382,14 +398,15 @@
         grad = dot_nn(pd[0:BLK, :], ycats[p]) * (invs[p] * factor)
         both = jnp.where(low, grad, obuf[p].astype(F32))
         bqo[p] = both.astype(BF16)
+        leave(Z_BQO, bqo, rqo, p)
         dtqo[:, pl.ds(pl.multiple_of(p * BLK, BLK), BLK)] = both.T.astype(BF16)
         return carry
 
     lax.fori_loop(0, PER, query_block, 0)
 
-    far = (0, 1, 3, 5, 7, 6, 4, 2)
-    rqo[z] = bqo[0]
-    c_bqo = [along(Z_BQO, d, bqo.at[far[d]], rqo.at[z]) for d in range(1, 8)]
+    c_bqo = left(Z_BQO, bqo, rqo)
+    x_far_pass(1, 2)
+    x_far_pass(1, 3)
     x_far_pass(1, 4)
 
     def stage1(k, part):
@@ -480,13 +497,13 @@
         g = dot_nn(pd[...], ycat[...])
         both = jnp.where(low, g[BLK : 2 * BLK] * factor, g[0:BLK])
         bkv[p] = both.astype(BF16)
+        leave(Z_BKV, bkv, rkv, p)
         dtkv[:, pl.ds(pl.multiple_of(p * BLK, BLK), BLK)] = both.T.astype(BF16)
         return carry
 
     lax.fori_loop(0, PER, key_block, 0)
 
-    rkv[z] = bkv[0]
-    c_bkv = [along(Z_BKV, d, bkv.at[far[d]], rkv.at[z]) for d in range(1, 8)]
+    c_bkv = left(Z_BKV, bkv, rkv)
     s1b = stage1(1, dot_nn(dtkv[...], hid[...].reshape(PER * BLK, D)))
     s2a = stage2(0, s1a)
 
@@ -517,8 +534,8 @@
         gp[:, tile(3 * g)] = jnp.where(low, qo_even, kv_even).astype(BF16)
         gp[:, tile(3 * g + 1)] = jnp.where(low, kv_even, swap(qo_odd)).astype(BF16)
         gp[:, tile(3 * g + 2)] = rkv[2 * g + 1]
+    s4b = stage4(1, s3b)
     grad_hidden = dot_nt(gp[...], wqkv[...])
-    s4b = stage4(1, s3b)
     normed = normed_ref[...]
     inner = jnp.mean(grad_hidden * normed, axis=-1, keepdims=True)
     gres[...] = ((grad_hidden - normed * inner) / spread_ref[...]).astype(BF16)
@@ -526,19 +543,29 @@
 
     for copy in s4a + s4b:
         copy.wait_recv()
-    first = fin[0].reshape(BLK, D).astype(F32)
-    second = fin[1].reshape(BLK, D).astype(F32)
-    gwo_ref[...] = first[HD : 2 * HD, :]
-    rows = jnp.concatenate([first[0:HD, :], second, jnp.zeros((HD, D), F32)], axis=0)
-    gqkv_ref[...] = rows.T[:, 0 : 3 * HD]
-
     for copy in pending:
         copy.wait_send()
     when(moved, lambda: [copy.wait_send() for copy in go] and None)
-    when(jnp.logical_not(moved), lambda: share.wait_send())
+    when(jnp.logical_not(moved), lambda: [copy.wait_send() for copy in share] and None)
     for here, there in (d_out, d_gtok):
         when(jnp.logical_not(moved), lambda: here.wait())
         when(moved, lambda: there.wait())
+
+
+def finish(out_in, gtok_in, fin_ref, out_hbm, gtok_hbm, gqkv_ref, gwo_ref, sems):
+    copies = [
+        pltpu.make_async_copy(out_in, out_hbm, sems.at[0]),
+        pltpu.make_async_copy(gtok_in, gtok_hbm, sems.at[1]),
+    ]
+    for copy in copies:
+        copy.start()
+    first = fin_ref[0].reshape(BLK, D).astype(F32)
+    second = fin_ref[1].reshape(BLK, D).astype(F32)
+    gwo_ref[...] = first[HD : 2 * HD, :]
+    gqkv_ref[0:HD, :] = first[0:HD, :]
+    gqkv_ref[HD : 3 * HD, :] = second
+    for copy in copies:
+        copy.wait()
 
 
 def body(tokens, bin_ids, pattern, w_qkv, w_out, head_bias, grad_output):
@@ -556,8 +583,9 @@
         half((BLK, D)),
         half((D, 3 * D)),
         half((D, D)),
-        pltpu.VMEM((NB + 8, BLK), jnp.int32),
-        pltpu.SMEM((8, BLK), jnp.int32),
+        pltpu.VMEM((1, NB * BLK), jnp.int32),
+        pltpu.VMEM((NNZ, 1, NB), jnp.int32),
+        pltpu.SMEM((NNZ, 1, NB), jnp.int32),
         half((D, 256)),
         half((BLK, D)),
         full((BLK, D)),
@@ -587,7 +615,6 @@
         half((2, 8, 16, D)),
         half((2, 4, 16, D)),
         half((2, 4, 16, D)),
-        half((2, 8, 16, D)),
         half((BLK, D)),
         half((BLK, 3 * D)),
         half((BLK, D)),
@@ -600,30 +627,38 @@
         dma((2, 2, 5, 2)),
         dma((2, 5, 7)),
         dma((2, 5, 7)),
-        dma((8,)),
-        dma((5,)),
-        dma((5,)),
+        dma((9,)),
+        dma((6,)),
+        dma((6,)),
     ]
-    aux = jnp.concatenate(
-        [bin_ids[0].reshape(NB, BLK), jnp.pad(pattern[0, 0:1], ((0, 7), (0, BLK - NNZ)))], axis=0
+    shapes = (
+        jax.ShapeDtypeStruct((BLK, D), BF16),
+        jax.ShapeDtypeStruct((BLK, D), BF16),
     )
+    parts = pl.pallas_call(
+        kernel,
+        out_shape=shapes + (jax.ShapeDtypeStruct((2, 8, 16, D), BF16),),
+        in_specs=[smem, hbm, hbm, hbm, hbm, hbm, hbm],
+        out_specs=(hbm, hbm, vmem),
+        scratch_shapes=scratch,
+        compiler_params=pltpu.CompilerParams(
+            collective_id=0, has_side_effects=True, vmem_limit_bytes=62 * 1024 * 1024
+        ),
+        name="layer",
+    )(head_bias, tokens[0], grad_output[0], w_qkv, w_out, bin_ids, pattern.transpose(2, 0, 1))
     result, grad_input, own_qkv, own_out = pl.pallas_call(
-        kernel,
-        out_shape=(
-            jax.ShapeDtypeStruct((BLK, D), BF16),
-            jax.ShapeDtypeStruct((BLK, D), BF16),
-            jax.ShapeDtypeStruct((D, 3 * HD), F32),
+        finish,
+        out_shape=shapes
+        + (
+            jax.ShapeDtypeStruct((3 * HD, D), F32),
             jax.ShapeDtypeStruct((HD, D), F32),
         ),
-        in_specs=[smem, hbm, hbm, hbm, hbm, hbm],
+        in_specs=[hbm, hbm, vmem],
         out_specs=(hbm, hbm, vmem, vmem),
-        scratch_shapes=scratch,
-        compiler_params=pltpu.CompilerParams(
-            collective_id=0, has_side_effects=True, vmem_limit_bytes=48 * 1024 * 1024
-        ),
-        name="layer",
-    )(head_bias, tokens[0], grad_output[0], w_qkv, w_out, aux)
-    return (result[None], grad_input[None], own_qkv, own_out)
+        scratch_shapes=[dma((2,))],
+        name="finish",
+    )(*parts)
+    return (result[None], grad_input[None], own_qkv.T, own_out)
 
 
 def solution(mesh):

time: 93.5 us -> 93.4 us (level)
  Pallas kernels: 83.1 us -> 92.6 us
  local copies, waits for them, and re-layouts: 8.76 us -> 0 us
    pallas_call x1 -> x2, Pallas kernels: 83.1 us -> 92.6 us  [the longest x1 81.8 us: body(): pl.pallas_call(kernel, out_shape=shapes + (jax.ShapeDtypeStruct((2, 8, 16...]
    unnamed x14 -> x0, local copies, waits for them, and re-layouts: 7.81 us -> none
    slice x1 -> x0, local copies, waits for them, and re-layouts: 0.95 us -> none  [body(): pattern[0, 0:1]]
where the time goes in v3:
time: 93.4 us; the launch traced here: 93.2 us
  Pallas kernels  92.6 us (99%)
    pallas_call x1, Pallas kernels, body(): pl.pallas_call(kernel, out_shape=shapes + (jax.ShapeDtypeStruct((2, 8, 16...  81.8 us
    pallas_call x1, Pallas kernels, body(): pl.pallas_call(finish, out_shape=shapes + (jax.ShapeDtypeStruct((3 * HD,...  10.8 us

profile of v3, /device:TPU:1, one launch (start us, length us, event | category | flops | bytes accessed | tf_op | source)
XLA Modules:
  0.0 93.2 jit_solution(1429929057095289693)
XLA Ops:
  0.6 81.8 %layer.1 = (bf16[128,512]{1,0:T(8,128)(2,1)}, bf16[128,512]{1,0:T(8,128)(2,1)}, bf16[2,8,16,512]{3,2,1,0:T(8,128)(2,1)}) custom-call(f32[8]{0:T(128)} %bias_ref.1, bf16[128,512]{1,0:T(8,128)(2,1)} %bitcast.6, bf16[128,512]{1,0:T(8,128)(2,1)} %bitcast.7, bf16[512,1536]{1,0:T(8,128)(2,1)} %wqkv_hbm.1, bf16[512,512]{1,0:T(8,128)(2,1)} %wout_hbm.1, ...), custom_call_target="tpu_custom_call" | custom-call | tf_op jit(solution)/shard_map/layer/pallas_call | solution.py:638
  82.4 10.8 %finish.1 = (bf16[128,512]{1,0:T(8,128)(2,1)}, bf16[128,512]{1,0:T(8,128)(2,1)}, f32[192,512]{1,0:T(8,128)}, f32[64,512]{1,0:T(8,128)}) custom-call(bf16[128,512]{1,0:T(8,128)(2,1)} %get-tuple-element.11.out_in, bf16[128,512]{1,0:T(8,128)(2,1)} %get-tuple-element.12.gtok_in, bf16[2,8,16,512]{3,2,1,0:T(8,128)(2,1)} %get-tuple-element.13.fin_ref), custom_call_target="tpu_custom_call" | custom-call | tf_op jit(solution)/shard_map/finish/pallas_call | solution.py:649

commit v4 on v3

--- a/solution.py
+++ b/solution.py
@@ -47,8 +47,8 @@
 
 def kernel(
     bias_ref, tok_hbm, gout_hbm, wqkv_hbm, wout_hbm, bins_hbm, pat_hbm,
-    out_hbm, gtok_hbm, fin,
-    gkv, gqd, hid, gog, tok, wqkv, wout, bins, patv, pat, wcat, wo2, normed_ref, spread_ref,
+    out_ref, gtok_ref, fin,
+    gkv, gqd, hid, gog, tok, tok_in, gout_in, bins_in, pat_in, wqkv, wout, bins, patv, pat, wcat, wo2, normed_ref, spread_ref,
     ycats, ycat, probs, sd, pd, a2, stcol, strow, stg, deltas, invs, binsf, binst,
     obuf, bqo, bkv, rqo, rkv, dtqo, dtkv,
     wpart, ars, arr, dpx, zbc, att, gp, res, gres,
@@ -123,23 +123,23 @@
         pltpu.make_async_copy(wqkv_hbm, wqkv, ins.at[0]),
         pltpu.make_async_copy(wout_hbm, wout, ins.at[1]),
     ]
-    stay = [
-        pltpu.make_async_copy(tok_hbm, tok, ins.at[2]),
-        pltpu.make_async_copy(gout_hbm, gog.at[0], ins.at[3]),
-        pltpu.make_async_copy(bins_hbm, bins, ins.at[4]),
-        pltpu.make_async_copy(pat_hbm, patv, ins.at[5]),
+    loads = [
+        pltpu.make_async_copy(tok_hbm, tok_in, ins.at[2]),
+        pltpu.make_async_copy(gout_hbm, gout_in, ins.at[3]),
+        pltpu.make_async_copy(bins_hbm, bins_in, ins.at[4]),
+        pltpu.make_async_copy(pat_hbm, pat_in, ins.at[5]),
     ]
     go = [
-        remote(tok_hbm, tok, sws.at[0], swr.at[0], partner),
-        remote(gout_hbm, gog.at[0], sws.at[1], swr.at[1], partner),
+        remote(tok_in, tok, sws.at[0], swr.at[0], partner),
+        remote(gout_in, gog.at[0], sws.at[1], swr.at[1], partner),
     ]
     share = [
-        remote(bins_hbm, bins, sws.at[2], swr.at[2], sibling),
-        remote(pat_hbm, patv, sws.at[5], swr.at[5], sibling),
+        remote(bins_in, bins, sws.at[2], swr.at[2], sibling),
+        remote(pat_in, patv, sws.at[5], swr.at[5], sibling),
     ]
-    for copy in weights:
+    for copy in loads + weights:
         copy.start()
-    when(jnp.logical_not(moved), lambda: [copy.start() for copy in stay] and None)
+    stays = jnp.logical_not(moved)
 
     lane = lax.broadcasted_iota(jnp.int32, (BLK, 2 * HD), 1)
     low = lane < HD
@@ -162,12 +162,23 @@
     wo2[0:HD, :] = jnp.zeros((HD, D), BF16)
     wo2[HD:BLK, :] = jnp.where(odd, wo_pair[HD:BLK, :], wo_pair[0:HD, :])
 
+    for copy in loads:
+        copy.wait()
+
+    def keep(dst, src):
+        def fn():
+            dst[...] = src[...]
+
+        when(stays, fn)
+
+    keep(tok, tok_in)
+    keep(gog.at[0], gout_in)
+    keep(bins, bins_in)
+    keep(patv, pat_in)
+
     pl.semaphore_wait(barrier, 17 + jnp.where(moved, 1, 0))
-    when(moved, lambda: [copy.start() for copy in go] and None)
-    when(jnp.logical_not(moved), lambda: [copy.start() for copy in share] and None)
-
+    when(moved, lambda: go[0].start())
     when(moved, lambda: go[0].wait_recv())
-    when(jnp.logical_not(moved), lambda: stay[0].wait())
 
     tokens = tok[...].astype(F32)
     spread = jnp.sqrt(jnp.mean(tokens * tokens, axis=-1, keepdims=True) + EPSILON)
@@ -259,36 +270,33 @@
         x_own(1, b)
 
     first_hop(0)
+    when(moved, lambda: go[1].start())
+    when(stays, lambda: [copy.start() for copy in share] and None)
     project(0)
-    when(moved, lambda: go[1].wait_recv())
-    when(jnp.logical_not(moved), lambda: stay[1].wait())
     next_hop(0, 1)
-    first_hop(1)
     project(1)
-    project_grad(0)
     next_hop(0, 2)
     project(2)
     x_pass(0, 0)
+    next_hop(0, 3)
+    when(moved, lambda: go[1].wait_recv())
+    first_hop(1)
+    project(3)
+    project_grad(0)
     x_pass(0, 1)
+    last_hop(0)
+    project(4)
+    x_far_pass(0, 0)
+    x_pass(0, 2)
+    x_far_pass(0, 1)
     next_hop(1, 1)
     project_grad(1)
-    next_hop(0, 3)
-    project(3)
-    x_far_pass(0, 0)
-    x_pass(0, 2)
-    x_pass(1, 0)
-    last_hop(0)
-    project(4)
-    next_hop(1, 2)
-    project_grad(2)
-    x_far_pass(0, 1)
     x_pass(0, 3)
     x_far_pass(0, 2)
     x_pass(0, 4)
-    x_pass(1, 1)
+    x_pass(1, 0)
 
     when(moved, lambda: [copy.wait_recv() for copy in share] and None)
-    when(jnp.logical_not(moved), lambda: [copy.wait() for copy in stay[2:]] and None)
     to_scalars = pltpu.make_async_copy(patv, pat, ins.at[8])
     to_scalars.start()
     for q in range(NB):
@@ -298,8 +306,9 @@
 
     x_far_pass(0, 3)
     x_far_pass(0, 4)
-    next_hop(1, 3)
-    project_grad(3)
+    next_hop(1, 2)
+    project_grad(2)
+    x_pass(1, 1)
     x_end(0)
 
     bias2 = bias_ref[z] * LOG2E
@@ -364,6 +373,8 @@
         return carry
 
     lax.fori_loop(0, PER, forward_block, 0)
+    next_hop(1, 3)
+    project_grad(3)
 
     last_hop(1)
     project_grad(4)
@@ -508,11 +519,10 @@
     s2a = stage2(0, s1a)
 
     def deliver(src, dst, k):
-        here = pltpu.make_async_copy(src, dst, ins.at[6 + k])
         there = remote(src, dst, sws.at[3 + k], swr.at[3 + k], partner)
-        when(jnp.logical_not(moved), lambda: here.start())
+        keep(dst, src)
         when(moved, lambda: there.start())
-        return here, there
+        return there
 
     for copy in c_bqo:
         copy.wait_recv()
@@ -520,7 +530,7 @@
         even, uneven = rqo[2 * g].astype(F32), rqo[2 * g + 1].astype(F32)
         att[:, tile(g)] = jnp.where(low, swap(even), uneven).astype(BF16)
     res[...] = dot_nn(att[...], wout[...]).astype(BF16)
-    d_out = deliver(res, out_hbm, 0)
+    d_out = deliver(res, out_ref, 0)
     s3a = stage3(0, s2a)
     s2b = stage2(1, s1b)
     s4a = stage4(0, s3a)
@@ -539,33 +549,26 @@
     normed = normed_ref[...]
     inner = jnp.mean(grad_hidden * normed, axis=-1, keepdims=True)
     gres[...] = ((grad_hidden - normed * inner) / spread_ref[...]).astype(BF16)
-    d_gtok = deliver(gres, gtok_hbm, 1)
+    d_gtok = deliver(gres, gtok_ref, 1)
 
     for copy in s4a + s4b:
         copy.wait_recv()
     for copy in pending:
         copy.wait_send()
     when(moved, lambda: [copy.wait_send() for copy in go] and None)
-    when(jnp.logical_not(moved), lambda: [copy.wait_send() for copy in share] and None)
-    for here, there in (d_out, d_gtok):
-        when(jnp.logical_not(moved), lambda: here.wait())
+    when(stays, lambda: [copy.wait_send() for copy in share] and None)
+    for there in (d_out, d_gtok):
         when(moved, lambda: there.wait())
 
 
-def finish(out_in, gtok_in, fin_ref, out_hbm, gtok_hbm, gqkv_ref, gwo_ref, sems):
-    copies = [
-        pltpu.make_async_copy(out_in, out_hbm, sems.at[0]),
-        pltpu.make_async_copy(gtok_in, gtok_hbm, sems.at[1]),
-    ]
-    for copy in copies:
-        copy.start()
+def finish(out_in, gtok_in, fin_ref, out_ref, gtok_ref, gqkv_ref, gwo_ref):
+    out_ref[...] = out_in[...]
+    gtok_ref[...] = gtok_in[...]
     first = fin_ref[0].reshape(BLK, D).astype(F32)
     second = fin_ref[1].reshape(BLK, D).astype(F32)
     gwo_ref[...] = first[HD : 2 * HD, :]
     gqkv_ref[0:HD, :] = first[0:HD, :]
     gqkv_ref[HD : 3 * HD, :] = second
-    for copy in copies:
-        copy.wait()
 
 
 def body(tokens, bin_ids, pattern, w_qkv, w_out, head_bias, grad_output):
@@ -581,6 +584,10 @@
         half((8, BLK, D)),
         half((8, BLK, D)),
         half((BLK, D)),
+        half((BLK, D)),
+        half((BLK, D)),
+        pltpu.VMEM((1, NB * BLK), jnp.int32),
+        pltpu.VMEM((NNZ, 1, NB), jnp.int32),
         half((D, 3 * D)),
         half((D, D)),
         pltpu.VMEM((1, NB * BLK), jnp.int32),
@@ -639,7 +646,7 @@
         kernel,
         out_shape=shapes + (jax.ShapeDtypeStruct((2, 8, 16, D), BF16),),
         in_specs=[smem, hbm, hbm, hbm, hbm, hbm, hbm],
-        out_specs=(hbm, hbm, vmem),
+        out_specs=(vmem, vmem, vmem),
         scratch_shapes=scratch,
         compiler_params=pltpu.CompilerParams(
             collective_id=0, has_side_effects=True, vmem_limit_bytes=62 * 1024 * 1024
@@ -653,9 +660,8 @@
             jax.ShapeDtypeStruct((3 * HD, D), F32),
             jax.ShapeDtypeStruct((HD, D), F32),
         ),
-        in_specs=[hbm, hbm, vmem],
-        out_specs=(hbm, hbm, vmem, vmem),
-        scratch_shapes=[dma((2,))],
+        in_specs=[vmem, vmem, vmem],
+        out_specs=(vmem, vmem, vmem, vmem),
         name="finish",
     )(*parts)
     return (result[None], grad_input[None], own_qkv.T, own_out)

time: 93.4 us -> 88.9 us (0.952)
  Pallas kernels: 92.6 us -> 88.1 us
    pallas_call x1, Pallas kernels: 10.8 us -> 1.97 us  [body(): pl.pallas_call(finish, out_shape=shapes + (jax.ShapeDtypeStruct((3 * HD,...]
    pallas_call x1, Pallas kernels: 81.8 us -> 86.1 us  [body(): pl.pallas_call(kernel, out_shape=shapes + (jax.ShapeDtypeStruct((2, 8, 16...]
where the time goes in v4:
time: 88.9 us; the launch traced here: 88.7 us
  Pallas kernels  88.1 us (99%)
    pallas_call x1, Pallas kernels, body(): pl.pallas_call(kernel, out_shape=shapes + (jax.ShapeDtypeStruct((2, 8, 16...  86.1 us
    pallas_call x1, Pallas kernels, body(): pl.pallas_call(finish, out_shape=shapes + (jax.ShapeDtypeStruct((3 * HD,...  1.97 us

profile of v4, /device:TPU:1, one launch (start us, length us, event | category | flops | bytes accessed | tf_op | source)
XLA Modules:
  0.0 88.7 jit_solution(8582531502284987462)
XLA Ops:
  0.6 86.1 %layer.1 = (bf16[128,512]{1,0:T(8,128)(2,1)}, bf16[128,512]{1,0:T(8,128)(2,1)}, bf16[2,8,16,512]{3,2,1,0:T(8,128)(2,1)}) custom-call(f32[8]{0:T(128)} %bias_ref.1, bf16[128,512]{1,0:T(8,128)(2,1)} %bitcast.6, bf16[128,512]{1,0:T(8,128)(2,1)} %bitcast.7, bf16[512,1536]{1,0:T(8,128)(2,1)} %wqkv_hbm.1, bf16[512,512]{1,0:T(8,128)(2,1)} %wout_hbm.1, ...), custom_call_target="tpu_custom_call" | custom-call | tf_op jit(solution)/shard_map/layer/pallas_call | solution.py:645
  86.7 2.0 %finish.1 = (bf16[128,512]{1,0:T(8,128)(2,1)}, bf16[128,512]{1,0:T(8,128)(2,1)}, f32[192,512]{1,0:T(8,128)}, f32[64,512]{1,0:T(8,128)}) custom-call(bf16[128,512]{1,0:T(8,128)(2,1)} %get-tuple-element.11.out_in, bf16[128,512]{1,0:T(8,128)(2,1)} %get-tuple-element.12.gtok_in, bf16[2,8,16,512]{3,2,1,0:T(8,128)(2,1)} %get-tuple-element.13.fin_ref), custom_call_target="tpu_custom_call" | custom-call | tf_op jit(solution)/shard_map/finish/pallas_call | solution.py:656

commit v5 on v4

--- a/solution.py
+++ b/solution.py
@@ -195,28 +195,33 @@
             src, dst = (0 if t == 1 else 2 * (t - 1)), (2 * t if t < 4 else 7)
         else:
             src, dst = (0 if t == 1 else 2 * (t - 1) - 1), 2 * t - 1
-        rows = pl.ds(64 * part, 64)
+        rows = pl.ds(32 * part, 32)
         return remote(
             rings[k].at[src, rows], rings[k].at[dst, rows],
             zs.at[k, way, t, part], zr.at[k, way, t, part],
             {"seq": mod8(z + 1) if way == 0 else mod8(z - 1)},
         )
 
+    orders = ((0, 1, 2, 3), (2, 3, 0, 1))
+
     def first_hop(k):
-        for part in (0, 1):
+        for i in range(4):
             for way in (0, 1):
+                part = orders[way][i]
                 table[k, way, 1, part] = start(hop(k, way, 1, part))
 
-    def next_hop(k, t):
-        for part in (0, 1):
+    def next_hop(k, t, turns=(0, 1, 2, 3)):
+        for i in turns:
             for way in (0, 1):
+                part = orders[way][i]
                 table[k, way, t, part].wait_recv()
-                if t + 1 < 4 or (t + 1 == 4 and part == way):
+                if t + 1 < 4 or i < 2:
                     table[k, way, t + 1, part] = start(hop(k, way, t + 1, part))
 
     def last_hop(k):
-        for way in (0, 1):
-            table[k, way, 4, way].wait_recv()
+        for i in (0, 1):
+            for way in (0, 1):
+                table[k, way, 4, orders[way][i]].wait_recv()
 
     pools = (gkv, gqd)
     ring_x = {}
@@ -234,14 +239,16 @@
         xcopy(k, b, 0, r, device(x_right, c))
         xcopy(k, b, 1, r, device(x_left, c))
         xcopy(k, b, 2, r, sibling)
+        if b >= 2:
+            xcopy(k, b, 5, r, device(x_far, c))
 
     def x_pass(k, b):
         ring_x[k, b, 0].wait_recv()
-        if b in (0, 1, 4):
+        if b == 0:
             xcopy(k, b, 5, 2 * x_left + c, device(x_right, c))
         xcopy(k, b, 3, 2 * x_left + c, sibling)
         ring_x[k, b, 1].wait_recv()
-        if b in (2, 3):
+        if b == 1:
             xcopy(k, b, 5, 2 * x_right + c, device(x_left, c))
         xcopy(k, b, 4, 2 * x_right + c, sibling)
 
@@ -273,28 +280,6 @@
     when(moved, lambda: go[1].start())
     when(stays, lambda: [copy.start() for copy in share] and None)
     project(0)
-    next_hop(0, 1)
-    project(1)
-    next_hop(0, 2)
-    project(2)
-    x_pass(0, 0)
-    next_hop(0, 3)
-    when(moved, lambda: go[1].wait_recv())
-    first_hop(1)
-    project(3)
-    project_grad(0)
-    x_pass(0, 1)
-    last_hop(0)
-    project(4)
-    x_far_pass(0, 0)
-    x_pass(0, 2)
-    x_far_pass(0, 1)
-    next_hop(1, 1)
-    project_grad(1)
-    x_pass(0, 3)
-    x_far_pass(0, 2)
-    x_pass(0, 4)
-    x_pass(1, 0)
 
     when(moved, lambda: [copy.wait_recv() for copy in share] and None)
     to_scalars = pltpu.make_async_copy(patv, pat, ins.at[8])
@@ -304,11 +289,34 @@
     binst[...] = jnp.concatenate([binsf[...], jnp.zeros((BLK - NB, BLK), F32)], axis=0).T
     to_scalars.wait()
 
+    next_hop(0, 1)
+    project(1)
+    next_hop(0, 2)
+    project(2)
+    x_pass(0, 0)
+    next_hop(0, 3, (0, 1))
+    when(moved, lambda: go[1].wait_recv())
+    first_hop(1)
+    next_hop(0, 3, (2, 3))
+    project(3)
+    x_pass(0, 1)
+    x_far_pass(0, 0)
+    last_hop(0)
+    project(4)
+    project_grad(0)
+    next_hop(1, 1)
+    project_grad(1)
+    x_pass(0, 2)
+    x_far_pass(0, 2)
+    x_pass(0, 3)
     x_far_pass(0, 3)
+    x_far_pass(0, 1)
+    next_hop(1, 2, (0, 1))
+    x_pass(0, 4)
     x_far_pass(0, 4)
-    next_hop(1, 2)
+    next_hop(1, 2, (2, 3))
     project_grad(2)
-    x_pass(1, 1)
+    x_pass(1, 0)
     x_end(0)
 
     bias2 = bias_ref[z] * LOG2E
@@ -343,7 +351,15 @@
 
     stcol[...] = jnp.zeros((BLK, BLK), F32)
 
+    def forward_grads():
+        for i in (0, 1):
+            for way in (0, 1):
+                part = orders[way][i]
+                hop(1, way, 3, part).wait_recv()
+                hop(1, way, 4, part).start()
+
     def forward_block(p, carry):
+        when(p == 2, forward_grads)
         row = own_block(p)
         for n in range(NNZ):
             _, rn, pn = used_block(row, n)
@@ -373,7 +389,12 @@
         return carry
 
     lax.fori_loop(0, PER, forward_block, 0)
-    next_hop(1, 3)
+    for i in (0, 1):
+        for way in (0, 1):
+            part = orders[way][i]
+            table[1, way, 4, part] = hop(1, way, 4, part)
+            pending.append(table[1, way, 4, part])
+            table[1, way, 3, orders[way][i + 2]].wait_recv()
     project_grad(3)
 
     last_hop(1)
@@ -392,11 +413,11 @@
         return start(remote(src, dst, ss.at[kind, d], rr.at[kind, d], device(*member(d))))
 
     c_st = [group(G_ST, d, mine, mine) for d in range(1, 8)]
+    x_pass(1, 1)
     x_far_pass(1, 0)
+    x_pass(1, 2)
+    x_far_pass(1, 2)
     x_far_pass(1, 1)
-    x_pass(1, 2)
-    x_pass(1, 3)
-    x_pass(1, 4)
 
     def query_block(p, carry):
         block = gqd[r, p]
@@ -416,8 +437,9 @@
     lax.fori_loop(0, PER, query_block, 0)
 
     c_bqo = left(Z_BQO, bqo, rqo)
-    x_far_pass(1, 2)
+    x_pass(1, 3)
     x_far_pass(1, 3)
+    x_pass(1, 4)
     x_far_pass(1, 4)
 
     def stage1(k, part):
@@ -531,10 +553,10 @@
         att[:, tile(g)] = jnp.where(low, swap(even), uneven).astype(BF16)
     res[...] = dot_nn(att[...], wout[...]).astype(BF16)
     d_out = deliver(res, out_ref, 0)
+    s2b = stage2(1, s1b)
     s3a = stage3(0, s2a)
-    s2b = stage2(1, s1b)
+    s3b = stage3(1, s2b)
     s4a = stage4(0, s3a)
-    s3b = stage3(1, s2b)
 
     for copy in c_bkv:
         copy.wait_recv()
@@ -544,12 +566,12 @@
         gp[:, tile(3 * g)] = jnp.where(low, qo_even, kv_even).astype(BF16)
         gp[:, tile(3 * g + 1)] = jnp.where(low, kv_even, swap(qo_odd)).astype(BF16)
         gp[:, tile(3 * g + 2)] = rkv[2 * g + 1]
-    s4b = stage4(1, s3b)
     grad_hidden = dot_nt(gp[...], wqkv[...])
     normed = normed_ref[...]
     inner = jnp.mean(grad_hidden * normed, axis=-1, keepdims=True)
     gres[...] = ((grad_hidden - normed * inner) / spread_ref[...]).astype(BF16)
     d_gtok = deliver(gres, gtok_ref, 1)
+    s4b = stage4(1, s3b)
 
     for copy in s4a + s4b:
         copy.wait_recv()
@@ -630,8 +652,8 @@
         dma((9, 8)),
         dma((2, 4)),
         dma((2, 4)),
-        dma((2, 2, 5, 2)),
-        dma((2, 2, 5, 2)),
+        dma((2, 2, 5, 4)),
+        dma((2, 2, 5, 4)),
         dma((2, 5, 7)),
         dma((2, 5, 7)),
         dma((9,)),

time: 88.9 us -> 86.1 us (0.969)
  Pallas kernels: 88.1 us -> 85.3 us
    pallas_call x1, Pallas kernels: 86.1 us -> 83.3 us  [body(): pl.pallas_call(kernel, out_shape=shapes + (jax.ShapeDtypeStruct((2, 8, 16...]
where the time goes in v5:
time: 86.1 us; the launch traced here: 85.9 us
  Pallas kernels  85.3 us (99%)
    pallas_call x1, Pallas kernels, body(): pl.pallas_call(kernel, out_shape=shapes + (jax.ShapeDtypeStruct((2, 8, 16...  83.3 us
    pallas_call x1, Pallas kernels, body(): pl.pallas_call(finish, out_shape=shapes + (jax.ShapeDtypeStruct((3 * HD,...  1.97 us

profile of v5, /device:TPU:1, one launch (start us, length us, event | category | flops | bytes accessed | tf_op | source)
XLA Modules:
  0.0 85.9 jit_solution(5176901924536192032)
XLA Ops:
  0.6 83.3 %layer.1 = (bf16[128,512]{1,0:T(8,128)(2,1)}, bf16[128,512]{1,0:T(8,128)(2,1)}, bf16[2,8,16,512]{3,2,1,0:T(8,128)(2,1)}) custom-call(f32[8]{0:T(128)} %bias_ref.1, bf16[128,512]{1,0:T(8,128)(2,1)} %bitcast.6, bf16[128,512]{1,0:T(8,128)(2,1)} %bitcast.7, bf16[512,1536]{1,0:T(8,128)(2,1)} %wqkv_hbm.1, bf16[512,512]{1,0:T(8,128)(2,1)} %wout_hbm.1, ...), custom_call_target="tpu_custom_call" | custom-call | tf_op jit(solution)/shard_map/layer/pallas_call | solution.py:667
  83.9 2.0 %finish.1 = (bf16[128,512]{1,0:T(8,128)(2,1)}, bf16[128,512]{1,0:T(8,128)(2,1)}, f32[192,512]{1,0:T(8,128)}, f32[64,512]{1,0:T(8,128)}) custom-call(bf16[128,512]{1,0:T(8,128)(2,1)} %get-tuple-element.11.out_in, bf16[128,512]{1,0:T(8,128)(2,1)} %get-tuple-element.12.gtok_in, bf16[2,8,16,512]{3,2,1,0:T(8,128)(2,1)} %get-tuple-element.13.fin_ref), custom_call_target="tpu_custom_call" | custom-call | tf_op jit(solution)/shard_map/finish/pallas_call | solution.py:678

commit v6 on v4

--- a/solution.py
+++ b/solution.py
@@ -178,6 +178,8 @@
 
     pl.semaphore_wait(barrier, 17 + jnp.where(moved, 1, 0))
     when(moved, lambda: go[0].start())
+    when(moved, lambda: go[0].wait_send())
+    when(moved, lambda: go[1].start())
     when(moved, lambda: go[0].wait_recv())
 
     tokens = tok[...].astype(F32)
@@ -211,7 +213,7 @@
         for part in (0, 1):
             for way in (0, 1):
                 table[k, way, t, part].wait_recv()
-                if t + 1 < 4 or (t + 1 == 4 and part == way):
+                if t + 1 < 4 or part == way:
                     table[k, way, t + 1, part] = start(hop(k, way, t + 1, part))
 
     def last_hop(k):
@@ -234,14 +236,16 @@
         xcopy(k, b, 0, r, device(x_right, c))
         xcopy(k, b, 1, r, device(x_left, c))
         xcopy(k, b, 2, r, sibling)
+        if b >= 2:
+            xcopy(k, b, 5, r, device(x_far, c))
 
     def x_pass(k, b):
         ring_x[k, b, 0].wait_recv()
-        if b in (0, 1, 4):
+        if b == 0:
             xcopy(k, b, 5, 2 * x_left + c, device(x_right, c))
         xcopy(k, b, 3, 2 * x_left + c, sibling)
         ring_x[k, b, 1].wait_recv()
-        if b in (2, 3):
+        if b == 1:
             xcopy(k, b, 5, 2 * x_right + c, device(x_left, c))
         xcopy(k, b, 4, 2 * x_right + c, sibling)
 
@@ -270,31 +274,11 @@
         x_own(1, b)
 
     first_hop(0)
-    when(moved, lambda: go[1].start())
     when(stays, lambda: [copy.start() for copy in share] and None)
     project(0)
-    next_hop(0, 1)
-    project(1)
-    next_hop(0, 2)
-    project(2)
-    x_pass(0, 0)
-    next_hop(0, 3)
     when(moved, lambda: go[1].wait_recv())
     first_hop(1)
-    project(3)
     project_grad(0)
-    x_pass(0, 1)
-    last_hop(0)
-    project(4)
-    x_far_pass(0, 0)
-    x_pass(0, 2)
-    x_far_pass(0, 1)
-    next_hop(1, 1)
-    project_grad(1)
-    x_pass(0, 3)
-    x_far_pass(0, 2)
-    x_pass(0, 4)
-    x_pass(1, 0)
 
     when(moved, lambda: [copy.wait_recv() for copy in share] and None)
     to_scalars = pltpu.make_async_copy(patv, pat, ins.at[8])
@@ -304,11 +288,40 @@
     binst[...] = jnp.concatenate([binsf[...], jnp.zeros((BLK - NB, BLK), F32)], axis=0).T
     to_scalars.wait()
 
-    x_far_pass(0, 3)
-    x_far_pass(0, 4)
+    next_hop(0, 1)
+    project(1)
+    x_pass(0, 0)
+    next_hop(1, 1)
+    project_grad(1)
+    x_far_pass(0, 0)
+    next_hop(0, 2)
+    project(2)
+    x_pass(0, 1)
+    x_pass(1, 0)
     next_hop(1, 2)
     project_grad(2)
+    x_far_pass(0, 1)
     x_pass(1, 1)
+    x_far_pass(1, 0)
+    next_hop(0, 3)
+    project(3)
+    x_pass(0, 2)
+    x_far_pass(0, 2)
+    x_far_pass(1, 1)
+    next_hop(1, 3)
+    project_grad(3)
+    last_hop(0)
+    project(4)
+    x_pass(1, 2)
+    x_far_pass(1, 2)
+    x_pass(0, 3)
+    x_far_pass(0, 3)
+    last_hop(1)
+    project_grad(4)
+    x_pass(0, 4)
+    x_far_pass(0, 4)
+    x_pass(1, 3)
+    x_far_pass(1, 3)
     x_end(0)
 
     bias2 = bias_ref[z] * LOG2E
@@ -373,11 +386,8 @@
         return carry
 
     lax.fori_loop(0, PER, forward_block, 0)
-    next_hop(1, 3)
-    project_grad(3)
-
-    last_hop(1)
-    project_grad(4)
+    x_pass(1, 4)
+    x_far_pass(1, 4)
 
     for p in range(PER):
         both = gqd[r, p].astype(F32) * obuf[p].astype(F32)
@@ -392,11 +402,6 @@
         return start(remote(src, dst, ss.at[kind, d], rr.at[kind, d], device(*member(d))))
 
     c_st = [group(G_ST, d, mine, mine) for d in range(1, 8)]
-    x_far_pass(1, 0)
-    x_far_pass(1, 1)
-    x_pass(1, 2)
-    x_pass(1, 3)
-    x_pass(1, 4)
 
     def query_block(p, carry):
         block = gqd[r, p]
@@ -416,9 +421,6 @@
     lax.fori_loop(0, PER, query_block, 0)
 
     c_bqo = left(Z_BQO, bqo, rqo)
-    x_far_pass(1, 2)
-    x_far_pass(1, 3)
-    x_far_pass(1, 4)
 
     def stage1(k, part):
         wpart[k] = part
@@ -531,10 +533,10 @@
         att[:, tile(g)] = jnp.where(low, swap(even), uneven).astype(BF16)
     res[...] = dot_nn(att[...], wout[...]).astype(BF16)
     d_out = deliver(res, out_ref, 0)
+    s2b = stage2(1, s1b)
     s3a = stage3(0, s2a)
-    s2b = stage2(1, s1b)
+    s3b = stage3(1, s2b)
     s4a = stage4(0, s3a)
-    s3b = stage3(1, s2b)
 
     for copy in c_bkv:
         copy.wait_recv()
@@ -544,18 +546,18 @@
         gp[:, tile(3 * g)] = jnp.where(low, qo_even, kv_even).astype(BF16)
         gp[:, tile(3 * g + 1)] = jnp.where(low, kv_even, swap(qo_odd)).astype(BF16)
         gp[:, tile(3 * g + 2)] = rkv[2 * g + 1]
-    s4b = stage4(1, s3b)
     grad_hidden = dot_nt(gp[...], wqkv[...])
     normed = normed_ref[...]
     inner = jnp.mean(grad_hidden * normed, axis=-1, keepdims=True)
     gres[...] = ((grad_hidden - normed * inner) / spread_ref[...]).astype(BF16)
     d_gtok = deliver(gres, gtok_ref, 1)
+    s4b = stage4(1, s3b)
 
     for copy in s4a + s4b:
         copy.wait_recv()
     for copy in pending:
         copy.wait_send()
-    when(moved, lambda: [copy.wait_send() for copy in go] and None)
+    when(moved, lambda: go[1].wait_send())
     when(stays, lambda: [copy.wait_send() for copy in share] and None)
     for there in (d_out, d_gtok):
         when(moved, lambda: there.wait())

time: 88.9 us -> 82.9 us (0.933)
  Pallas kernels: 88.1 us -> 82.1 us
    pallas_call x1, Pallas kernels: 86.1 us -> 80.1 us  [body(): pl.pallas_call(kernel, out_shape=shapes + (jax.ShapeDtypeStruct((2, 8, 16...]
where the time goes in v6:
time: 82.9 us; the launch traced here: 82.7 us
  Pallas kernels  82.1 us (99%)
    pallas_call x1, Pallas kernels, body(): pl.pallas_call(kernel, out_shape=shapes + (jax.ShapeDtypeStruct((2, 8, 16...  80.1 us
    pallas_call x1, Pallas kernels, body(): pl.pallas_call(finish, out_shape=shapes + (jax.ShapeDtypeStruct((3 * HD,...  1.97 us

profile of v6, /device:TPU:1, one launch (start us, length us, event | category | flops | bytes accessed | tf_op | source)
XLA Modules:
  0.0 82.7 jit_solution(5634570862778591702)
XLA Ops:
  0.6 80.1 %layer.1 = (bf16[128,512]{1,0:T(8,128)(2,1)}, bf16[128,512]{1,0:T(8,128)(2,1)}, bf16[2,8,16,512]{3,2,1,0:T(8,128)(2,1)}) custom-call(f32[8]{0:T(128)} %bias_ref.1, bf16[128,512]{1,0:T(8,128)(2,1)} %bitcast.6, bf16[128,512]{1,0:T(8,128)(2,1)} %bitcast.7, bf16[512,1536]{1,0:T(8,128)(2,1)} %wqkv_hbm.1, bf16[512,512]{1,0:T(8,128)(2,1)} %wout_hbm.1, ...), custom_call_target="tpu_custom_call" | custom-call | tf_op jit(solution)/shard_map/layer/pallas_call | solution.py:647
  80.8 2.0 %finish.1 = (bf16[128,512]{1,0:T(8,128)(2,1)}, bf16[128,512]{1,0:T(8,128)(2,1)}, f32[192,512]{1,0:T(8,128)}, f32[64,512]{1,0:T(8,128)}) custom-call(bf16[128,512]{1,0:T(8,128)(2,1)} %get-tuple-element.11.out_in, bf16[128,512]{1,0:T(8,128)(2,1)} %get-tuple-element.12.gtok_in, bf16[2,8,16,512]{3,2,1,0:T(8,128)(2,1)} %get-tuple-element.13.fin_ref), custom_call_target="tpu_custom_call" | custom-call | tf_op jit(solution)/shard_map/finish/pallas_call | solution.py:658

commit v7 on v6

--- a/solution.py
+++ b/solution.py
@@ -52,7 +52,7 @@
     ycats, ycat, probs, sd, pd, a2, stcol, strow, stg, deltas, invs, binsf, binst,
     obuf, bqo, bkv, rqo, rkv, dtqo, dtkv,
     wpart, ars, arr, dpx, zbc, att, gp, res, gres,
-    ss, rr, ys, yr, zs, zr, xs, xr, ins, sws, swr,
+    ss, rr, ys, yr, zs, zr, xs, xr, xe, ins, sws, swr,
 ):
     dp = lax.axis_index("dp")
     z = lax.axis_index("seq")
@@ -93,12 +93,12 @@
             device_id=dev, device_id_type=MESH,
         )
 
-    pending = []
-
     def start(copy):
         copy.start()
-        pending.append(copy)
         return copy
+
+    def wait_bytes(ref, sem):
+        pltpu.make_async_copy(ref, ref, sem).wait()
 
     def when(cond, fn):
         pl.when(cond)(fn)
@@ -200,7 +200,7 @@
         rows = pl.ds(64 * part, 64)
         return remote(
             rings[k].at[src, rows], rings[k].at[dst, rows],
-            zs.at[k, way, t, part], zr.at[k, way, t, part],
+            zs.at[k], zr.at[k, way, t - 1, part],
             {"seq": mod8(z + 1) if way == 0 else mod8(z - 1)},
         )
 
@@ -225,12 +225,13 @@
     x_right, x_left = lax.rem(x + 1, 4), lax.rem(x + 3, 4)
     x_far = lax.rem(x + 2, 4)
 
+    gates = {0: 0, 1: 1, 5: 2}
+
     def xcopy(k, b, kind, owner, dev):
         first, count = BATCHES[b]
         part = pools[k].at[owner, pl.ds(first, count)]
-        ring_x[k, b, kind] = start(
-            remote(part, part, xs.at[k, b, kind], xr.at[k, b, kind], dev)
-        )
+        rsem = xr.at[k, b, gates[kind]] if kind in gates else xe.at[k]
+        ring_x[k, b, kind] = start(remote(part, part, xs.at[k], rsem, dev))
 
     def x_own(k, b):
         xcopy(k, b, 0, r, device(x_right, c))
@@ -254,9 +255,7 @@
         xcopy(k, b, 6, 2 * x_far + c, sibling)
 
     def x_end(k):
-        for b in range(5):
-            for kind in (2, 3, 4, 6):
-                ring_x[k, b, kind].wait_recv()
+        wait_bytes(pools[k].at[pl.ds(0, 4)], xe.at[k])
 
     def project(b):
         first, count = BATCHES[b]
@@ -333,19 +332,11 @@
     def own_block(p):
         return 8 * mod8(z + distance(p)) + r
 
-    far = (0, 1, 3, 5, 7, 6, 4, 2)
-
     def back(kind, src, dst, d):
-        return remote(src, dst, ss.at[kind, d], rr.at[kind, d], {"seq": mod8(z + d)})
+        return remote(src, dst, ss.at[kind], rr.at[kind], {"seq": mod8(z + d)})
 
     def leave(kind, buf, dst, p):
         when(p > 0, lambda: back(kind, buf.at[p], dst.at[z], distance(p)).start())
-
-    def left(kind, buf, dst):
-        dst[z] = buf[0]
-        copies = [back(kind, buf.at[far[d]], dst.at[z], d) for d in range(1, 8)]
-        pending.extend(copies)
-        return copies
 
     def used_block(row, n):
         other = lax.rem(row + pat[n, 0, 0], NB)
@@ -399,9 +390,10 @@
     stg[pl.ds(pl.multiple_of(2 * PER * r, 16), 16), :] = strow[0:16, :]
 
     def group(kind, d, src, dst):
-        return start(remote(src, dst, ss.at[kind, d], rr.at[kind, d], device(*member(d))))
-
-    c_st = [group(G_ST, d, mine, mine) for d in range(1, 8)]
+        start(remote(src, dst, ss.at[kind], rr.at[kind], device(*member(d))))
+
+    for d in range(1, 8):
+        group(G_ST, d, mine, mine)
 
     def query_block(p, carry):
         block = gqd[r, p]
@@ -420,71 +412,60 @@
 
     lax.fori_loop(0, PER, query_block, 0)
 
-    c_bqo = left(Z_BQO, bqo, rqo)
+    rqo[z] = bqo[0]
 
     def stage1(k, part):
         wpart[k] = part
         for q in range(8):
             ars[k, q] = part[16 * q : 16 * (q + 1), :].astype(BF16)
-        sent = []
         for d in range(1, 8):
             xx, cc = member(d)
-            sent.append(group((G_S1A, G_S1B)[k], d, ars.at[k, 2 * xx + cc], arr.at[k, r]))
-        return sent
-
-    def stage2(k, copies):
+            group((G_S1A, G_S1B)[k], d, ars.at[k, 2 * xx + cc], arr.at[k, r])
+
+    def stage2(k):
+        wait_bytes(arr.at[k, pl.ds(0, 7)], rr.at[(G_S1A, G_S1B)[k]])
         total = wpart[k, pl.ds(pl.multiple_of(16 * r, 16), 16), :]
-        for d, copy in zip(range(1, 8), copies):
-            copy.wait_recv()
+        for d in range(1, 8):
             total = total + arr[k, giver(d)].astype(F32)
         dpx[k, seqno] = total.astype(BF16)
         slot = dpx.at[k, seqno]
-        return [
-            start(remote(slot, slot, ys.at[k, e], yr.at[k, e], others[e - 1]))
-            for e in range(1, 4)
-        ]
+        for e in range(1, 4):
+            start(remote(slot, slot, ys.at[k], yr.at[k], others[e - 1]))
 
     mine_here = lax.rem(z, 2) == ylo
-
-    def stage3(k, copies):
-        for copy in copies:
-            copy.wait_recv()
+    not_here = jnp.logical_not(mine_here)
+
+    def stage3(k):
+        wait_bytes(dpx.at[k, pl.ds(0, 3)], yr.at[k])
         total = dpx[k, 0].astype(F32)
         for q in range(1, 4):
             total = total + dpx[k, q].astype(F32)
+        slot = zbc.at[k, z // 2]
+        kind = (Z_S3A, Z_S3B)[k]
 
         def spread_out():
             zbc[k, z // 2] = total.astype(BF16)
-
-        slot = zbc.at[k, z // 2]
+            for d in range(1, 8):
+                remote(slot, slot, ss.at[kind], rr.at[kind], {"seq": mod8(z + d)}).start()
+
+        when(mine_here, spread_out)
+
+    def stage4(k):
         kind = (Z_S3A, Z_S3B)[k]
-        sent = [
-            remote(slot, slot, ss.at[kind, d], rr.at[kind, d], {"seq": mod8(z + d)})
-            for d in range(1, 8)
-        ]
-        when(mine_here, spread_out)
-        when(mine_here, lambda: [copy.start() for copy in sent] and None)
-        return sent
-
-    def stage4(k, copies):
-        for d, copy in zip(range(1, 8), copies):
-            when(lax.rem(z + 8 - d, 2) == ylo, lambda: copy.wait_recv())
+        when(mine_here, lambda: wait_bytes(zbc.at[k, pl.ds(0, 3)], rr.at[kind]))
+        when(not_here, lambda: wait_bytes(zbc.at[k, pl.ds(0, 4)], rr.at[kind]))
         fin[k, r] = zbc[k, x]
-        sent = []
         for d in range(1, 8):
             xx, _ = member(d)
-            sent.append(group((G_S4A, G_S4B)[k], d, zbc.at[k, xx], fin.at[k, r]))
-        when(mine_here, lambda: [copy.wait_send() for copy in copies] and None)
-        return sent
+            group((G_S4A, G_S4B)[k], d, zbc.at[k, xx], fin.at[k, r])
 
     hid_all = hid[...].reshape(PER * BLK, D)
     go_all = gog[...].reshape(PER * BLK, D)
     part0 = jnp.concatenate(
         [dot_nn(dtqo[0:HD, :], hid_all), dot_nn(dtqo[HD : 2 * HD, :], go_all)], axis=0
     )
-    s1a = stage1(0, part0)
-    for copy in c_st:
-        copy.wait_recv()
+    stage1(0, part0)
+    wait_bytes(stg.at[pl.ds(0, 7 * 16)], rr.at[G_ST])
     x_end(1)
 
     def key_block(p, carry):
@@ -516,9 +497,9 @@
 
     lax.fori_loop(0, PER, key_block, 0)
 
-    c_bkv = left(Z_BKV, bkv, rkv)
-    s1b = stage1(1, dot_nn(dtkv[...], hid[...].reshape(PER * BLK, D)))
-    s2a = stage2(0, s1a)
+    rkv[z] = bkv[0]
+    stage1(1, dot_nn(dtkv[...], hid[...].reshape(PER * BLK, D)))
+    stage2(0)
 
     def deliver(src, dst, k):
         there = remote(src, dst, sws.at[3 + k], swr.at[3 + k], partner)
@@ -526,20 +507,18 @@
         when(moved, lambda: there.start())
         return there
 
-    for copy in c_bqo:
-        copy.wait_recv()
+    wait_bytes(rqo.at[pl.ds(0, 7)], rr.at[Z_BQO])
     for g in range(HEADS // 2):
         even, uneven = rqo[2 * g].astype(F32), rqo[2 * g + 1].astype(F32)
         att[:, tile(g)] = jnp.where(low, swap(even), uneven).astype(BF16)
     res[...] = dot_nn(att[...], wout[...]).astype(BF16)
     d_out = deliver(res, out_ref, 0)
-    s2b = stage2(1, s1b)
-    s3a = stage3(0, s2a)
-    s3b = stage3(1, s2b)
-    s4a = stage4(0, s3a)
-
-    for copy in c_bkv:
-        copy.wait_recv()
+    stage2(1)
+    stage3(0)
+    stage3(1)
+    stage4(0)
+
+    wait_bytes(rkv.at[pl.ds(0, 7)], rr.at[Z_BKV])
     for g in range(HEADS // 2):
         qo_even, qo_odd = rqo[2 * g].astype(F32), rqo[2 * g + 1].astype(F32)
         kv_even = swap(rkv[2 * g].astype(F32))
@@ -551,12 +530,25 @@
     inner = jnp.mean(grad_hidden * normed, axis=-1, keepdims=True)
     gres[...] = ((grad_hidden - normed * inner) / spread_ref[...]).astype(BF16)
     d_gtok = deliver(gres, gtok_ref, 1)
-    s4b = stage4(1, s3b)
-
-    for copy in s4a + s4b:
-        copy.wait_recv()
-    for copy in pending:
-        copy.wait_send()
+    stage4(1)
+
+    for k in (0, 1):
+        wait_bytes(fin.at[k, pl.ds(0, 7)], rr.at[(G_S4A, G_S4B)[k]])
+    for k in (0, 1):
+        wait_bytes(rings[k].at[pl.ds(0, 7)], zs.at[k])
+        wait_bytes(pools[k].at[pl.ds(0, 7)], xs.at[k])
+        wait_bytes(dpx.at[k, pl.ds(0, 3)], ys.at[k])
+        wait_bytes(arr.at[k, pl.ds(0, 7)], ss.at[(G_S1A, G_S1B)[k]])
+        wait_bytes(arr.at[k, pl.ds(0, 7)], ss.at[(G_S4A, G_S4B)[k]])
+    wait_bytes(rqo.at[pl.ds(0, 7)], ss.at[Z_BQO])
+    wait_bytes(rkv.at[pl.ds(0, 7)], ss.at[Z_BKV])
+    wait_bytes(stg.at[pl.ds(0, 7 * 16)], ss.at[G_ST])
+
+    def spread_sent():
+        for kind in (Z_S3A, Z_S3B):
+            wait_bytes(arr.at[0, pl.ds(0, 7)], ss.at[kind])
+
+    when(mine_here, spread_sent)
     when(moved, lambda: go[1].wait_send())
     when(stays, lambda: [copy.wait_send() for copy in share] and None)
     for there in (d_out, d_gtok):
@@ -628,14 +620,15 @@
         half((BLK, 3 * D)),
         half((BLK, D)),
         half((BLK, D)),
-        dma((9, 8)),
-        dma((9, 8)),
-        dma((2, 4)),
-        dma((2, 4)),
-        dma((2, 2, 5, 2)),
-        dma((2, 2, 5, 2)),
-        dma((2, 5, 7)),
-        dma((2, 5, 7)),
+        dma((9,)),
+        dma((9,)),
+        dma((2,)),
+        dma((2,)),
+        dma((2,)),
+        dma((2, 2, 4, 2)),
+        dma((2,)),
+        dma((2, 5, 3)),
+        dma((2,)),
         dma((9,)),
         dma((6,)),
         dma((6,)),

time: 82.9 us -> 80 us (0.965)
  Pallas kernels: 82.1 us -> 79.2 us
    pallas_call x1, Pallas kernels: 80.1 us -> 77.3 us  [body(): pl.pallas_call(kernel, out_shape=shapes + (jax.ShapeDtypeStruct((2, 8, 16...]
where the time goes in v7:
time: 80 us; the launch traced here: 79.9 us
  Pallas kernels  79.2 us (99%)
    pallas_call x1, Pallas kernels, body(): pl.pallas_call(kernel, out_shape=shapes + (jax.ShapeDtypeStruct((2, 8, 16...  77.3 us
    pallas_call x1, Pallas kernels, body(): pl.pallas_call(finish, out_shape=shapes + (jax.ShapeDtypeStruct((3 * HD,...  1.97 us

profile of v7, /device:TPU:1, one launch (start us, length us, event | category | flops | bytes accessed | tf_op | source)
XLA Modules:
  0.0 79.9 jit_solution(13561749461311273616)
XLA Ops:
  0.6 77.3 %layer.1 = (bf16[128,512]{1,0:T(8,128)(2,1)}, bf16[128,512]{1,0:T(8,128)(2,1)}, bf16[2,8,16,512]{3,2,1,0:T(8,128)(2,1)}) custom-call(f32[8]{0:T(128)} %bias_ref.1, bf16[128,512]{1,0:T(8,128)(2,1)} %bitcast.6, bf16[128,512]{1,0:T(8,128)(2,1)} %bitcast.7, bf16[512,1536]{1,0:T(8,128)(2,1)} %wqkv_hbm.1, bf16[512,512]{1,0:T(8,128)(2,1)} %wout_hbm.1, ...), custom_call_target="tpu_custom_call" | custom-call | tf_op jit(solution)/shard_map/layer/pallas_call | solution.py:640
  77.9 2.0 %finish.1 = (bf16[128,512]{1,0:T(8,128)(2,1)}, bf16[128,512]{1,0:T(8,128)(2,1)}, f32[192,512]{1,0:T(8,128)}, f32[64,512]{1,0:T(8,128)}) custom-call(bf16[128,512]{1,0:T(8,128)(2,1)} %get-tuple-element.11.out_in, bf16[128,512]{1,0:T(8,128)(2,1)} %get-tuple-element.12.gtok_in, bf16[2,8,16,512]{3,2,1,0:T(8,128)(2,1)} %get-tuple-element.13.fin_ref), custom_call_target="tpu_custom_call" | custom-call | tf_op jit(solution)/shard_map/finish/pallas_call | solution.py:651

commit v8 on v7

--- a/solution.py
+++ b/solution.py
@@ -108,9 +108,11 @@
     def greet(dev):
         pl.semaphore_signal(barrier, inc=1, device_id=dev, device_id_type=MESH)
 
-    for d in range(1, 8):
+    for d in (1, 7):
         greet({"seq": mod8(z + d)})
-        greet(device(*member(d)))
+    for d in (1, 2, 3):
+        greet(device(lax.rem(x + d, 4), c))
+    greet(sibling)
     others = []
     for e in range(1, 4):
         yh = yhi if e // 2 == 0 else 1 - yhi
@@ -176,7 +178,7 @@
     keep(bins, bins_in)
     keep(patv, pat_in)
 
-    pl.semaphore_wait(barrier, 17 + jnp.where(moved, 1, 0))
+    pl.semaphore_wait(barrier, 9 + jnp.where(moved, 1, 0))
     when(moved, lambda: go[0].start())
     when(moved, lambda: go[0].wait_send())
     when(moved, lambda: go[1].start())

time: 80 us -> 78.9 us (0.986)
  Pallas kernels: 79.2 us -> 78.2 us
    pallas_call x1, Pallas kernels: 77.3 us -> 76.2 us  [body(): pl.pallas_call(kernel, out_shape=shapes + (jax.ShapeDtypeStruct((2, 8, 16...]
where the time goes in v8:
time: 78.9 us; the launch traced here: 78.8 us
  Pallas kernels  78.2 us (99%)
    pallas_call x1, Pallas kernels, body(): pl.pallas_call(kernel, out_shape=shapes + (jax.ShapeDtypeStruct((2, 8, 16...  76.2 us
    pallas_call x1, Pallas kernels, body(): pl.pallas_call(finish, out_shape=shapes + (jax.ShapeDtypeStruct((3 * HD,...  1.97 us

profile of v8, /device:TPU:1, one launch (start us, length us, event | category | flops | bytes accessed | tf_op | source)
XLA Modules:
  0.0 78.8 jit_solution(1931434399707694348)
XLA Ops:
  0.6 76.2 %layer.1 = (bf16[128,512]{1,0:T(8,128)(2,1)}, bf16[128,512]{1,0:T(8,128)(2,1)}, bf16[2,8,16,512]{3,2,1,0:T(8,128)(2,1)}) custom-call(f32[8]{0:T(128)} %bias_ref.1, bf16[128,512]{1,0:T(8,128)(2,1)} %bitcast.6, bf16[128,512]{1,0:T(8,128)(2,1)} %bitcast.7, bf16[512,1536]{1,0:T(8,128)(2,1)} %wqkv_hbm.1, bf16[512,512]{1,0:T(8,128)(2,1)} %wout_hbm.1, ...), custom_call_target="tpu_custom_call" | custom-call | tf_op jit(solution)/shard_map/layer/pallas_call | solution.py:642
  76.8 2.0 %finish.1 = (bf16[128,512]{1,0:T(8,128)(2,1)}, bf16[128,512]{1,0:T(8,128)(2,1)}, f32[192,512]{1,0:T(8,128)}, f32[64,512]{1,0:T(8,128)}) custom-call(bf16[128,512]{1,0:T(8,128)(2,1)} %get-tuple-element.11.out_in, bf16[128,512]{1,0:T(8,128)(2,1)} %get-tuple-element.12.gtok_in, bf16[2,8,16,512]{3,2,1,0:T(8,128)(2,1)} %get-tuple-element.13.fin_ref), custom_call_target="tpu_custom_call" | custom-call | tf_op jit(solution)/shard_map/finish/pallas_call | solution.py:653

commit v9 on v8

--- a/solution.py
+++ b/solution.py
@@ -112,6 +112,7 @@
         greet({"seq": mod8(z + d)})
     for d in (1, 2, 3):
         greet(device(lax.rem(x + d, 4), c))
+        greet(device(lax.rem(x + d, 4), 1 - c))
     greet(sibling)
     others = []
     for e in range(1, 4):
@@ -131,10 +132,12 @@
         pltpu.make_async_copy(bins_hbm, bins_in, ins.at[4]),
         pltpu.make_async_copy(pat_hbm, pat_in, ins.at[5]),
     ]
-    go = [
-        remote(tok_in, tok, sws.at[0], swr.at[0], partner),
-        remote(gout_in, gog.at[0], sws.at[1], swr.at[1], partner),
+    halves = [pl.ds(0, 64), pl.ds(64, 64)]
+    go_tok = [
+        remote(tok_in.at[rows], tok.at[rows], sws.at[sem], swr.at[sem], partner)
+        for rows, sem in zip(halves, (0, 6))
     ]
+    go_grad = remote(gout_in, gog.at[0], sws.at[1], swr.at[1], partner)
     share = [
         remote(bins_in, bins, sws.at[2], swr.at[2], sibling),
         remote(pat_in, patv, sws.at[5], swr.at[5], sibling),
@@ -178,18 +181,15 @@
     keep(bins, bins_in)
     keep(patv, pat_in)
 
-    pl.semaphore_wait(barrier, 9 + jnp.where(moved, 1, 0))
-    when(moved, lambda: go[0].start())
-    when(moved, lambda: go[0].wait_send())
-    when(moved, lambda: go[1].start())
-    when(moved, lambda: go[0].wait_recv())
-
-    tokens = tok[...].astype(F32)
-    spread = jnp.sqrt(jnp.mean(tokens * tokens, axis=-1, keepdims=True) + EPSILON)
-    normed = tokens / spread
-    normed_ref[...] = normed
-    spread_ref[...] = spread
-    hid[0] = normed.astype(BF16)
+    pl.semaphore_wait(barrier, 12 + jnp.where(moved, 1, 0))
+
+    def exchange():
+        for copy in go_tok:
+            copy.start()
+            copy.wait_send()
+        go_grad.start()
+
+    when(moved, exchange)
 
     rings = (hid, gog)
     table = {}
@@ -241,20 +241,27 @@
         xcopy(k, b, 2, r, sibling)
         if b >= 2:
             xcopy(k, b, 5, r, device(x_far, c))
+        if b == 4:
+            xcopy(k, b, 3, r, device(x_right, 1 - c))
+            xcopy(k, b, 4, r, device(x_left, 1 - c))
+            xcopy(k, b, 6, r, device(x_far, 1 - c))
 
     def x_pass(k, b):
         ring_x[k, b, 0].wait_recv()
         if b == 0:
             xcopy(k, b, 5, 2 * x_left + c, device(x_right, c))
-        xcopy(k, b, 3, 2 * x_left + c, sibling)
+        if b < 4:
+            xcopy(k, b, 3, 2 * x_left + c, sibling)
         ring_x[k, b, 1].wait_recv()
         if b == 1:
             xcopy(k, b, 5, 2 * x_right + c, device(x_left, c))
-        xcopy(k, b, 4, 2 * x_right + c, sibling)
+        if b < 4:
+            xcopy(k, b, 4, 2 * x_right + c, sibling)
 
     def x_far_pass(k, b):
         ring_x[k, b, 5].wait_recv()
-        xcopy(k, b, 6, 2 * x_far + c, sibling)
+        if b < 4:
+            xcopy(k, b, 6, 2 * x_far + c, sibling)
 
     def x_end(k):
         wait_bytes(pools[k].at[pl.ds(0, 4)], xe.at[k])
@@ -274,10 +281,19 @@
             gqd[r, p] = jnp.where(low, gqd[r, p], u.astype(BF16))
         x_own(1, b)
 
-    first_hop(0)
+    for part, rows in enumerate(halves):
+        when(moved, lambda: go_tok[part].wait_recv())
+        tokens = tok[rows, :].astype(F32)
+        spread = jnp.sqrt(jnp.mean(tokens * tokens, axis=-1, keepdims=True) + EPSILON)
+        normed = tokens / spread
+        normed_ref[rows, :] = normed
+        spread_ref[rows, :] = spread
+        hid[0, rows, :] = normed.astype(BF16)
+        for way in (0, 1):
+            table[0, way, 1, part] = start(hop(0, way, 1, part))
     when(stays, lambda: [copy.start() for copy in share] and None)
     project(0)
-    when(moved, lambda: go[1].wait_recv())
+    when(moved, lambda: go_grad.wait_recv())
     first_hop(1)
     project_grad(0)
 
@@ -551,7 +567,7 @@
             wait_bytes(arr.at[0, pl.ds(0, 7)], ss.at[kind])
 
     when(mine_here, spread_sent)
-    when(moved, lambda: go[1].wait_send())
+    when(moved, lambda: go_grad.wait_send())
     when(stays, lambda: [copy.wait_send() for copy in share] and None)
     for there in (d_out, d_gtok):
         when(moved, lambda: there.wait())
@@ -632,8 +648,8 @@
         dma((2, 5, 3)),
         dma((2,)),
         dma((9,)),
-        dma((6,)),
-        dma((6,)),
+        dma((7,)),
+        dma((7,)),
     ]
     shapes = (
         jax.ShapeDtypeStruct((BLK, D), BF16),

time: 78.9 us -> 80.9 us (1.025)
  Pallas kernels: 78.2 us -> 80.1 us
    pallas_call x1, Pallas kernels: 76.2 us -> 78.1 us  [body(): pl.pallas_call(kernel, out_shape=shapes + (jax.ShapeDtypeStruct((2, 8, 16...]
where the time goes in v9:
time: 80.9 us; the launch traced here: 80.7 us
  Pallas kernels  80.1 us (99%)
    pallas_call x1, Pallas kernels, body(): pl.pallas_call(kernel, out_shape=shapes + (jax.ShapeDtypeStruct((2, 8, 16...  78.1 us
    pallas_call x1, Pallas kernels, body(): pl.pallas_call(finish, out_shape=shapes + (jax.ShapeDtypeStruct((3 * HD,...  1.97 us

profile of v9, /device:TPU:1, one launch (start us, length us, event | category | flops | bytes accessed | tf_op | source)
XLA Modules:
  0.0 80.7 jit_solution(10890787152373387617)
XLA Ops:
  0.6 78.1 %layer.1 = (bf16[128,512]{1,0:T(8,128)(2,1)}, bf16[128,512]{1,0:T(8,128)(2,1)}, bf16[2,8,16,512]{3,2,1,0:T(8,128)(2,1)}) custom-call(f32[8]{0:T(128)} %bias_ref.1, bf16[128,512]{1,0:T(8,128)(2,1)} %bitcast.6, bf16[128,512]{1,0:T(8,128)(2,1)} %bitcast.7, bf16[512,1536]{1,0:T(8,128)(2,1)} %wqkv_hbm.1, bf16[512,512]{1,0:T(8,128)(2,1)} %wout_hbm.1, ...), custom_call_target="tpu_custom_call" | custom-call | tf_op jit(solution)/shard_map/layer/pallas_call | solution.py:658
  78.8 2.0 %finish.1 = (bf16[128,512]{1,0:T(8,128)(2,1)}, bf16[128,512]{1,0:T(8,128)(2,1)}, f32[192,512]{1,0:T(8,128)}, f32[64,512]{1,0:T(8,128)}) custom-call(bf16[128,512]{1,0:T(8,128)(2,1)} %get-tuple-element.11.out_in, bf16[128,512]{1,0:T(8,128)(2,1)} %get-tuple-element.12.gtok_in, bf16[2,8,16,512]{3,2,1,0:T(8,128)(2,1)} %get-tuple-element.13.fin_ref), custom_call_target="tpu_custom_call" | custom-call | tf_op jit(solution)/shard_map/finish/pallas_call | solution.py:669

commit v10 on v8

--- a/solution.py
+++ b/solution.py
@@ -239,17 +239,12 @@
         xcopy(k, b, 0, r, device(x_right, c))
         xcopy(k, b, 1, r, device(x_left, c))
         xcopy(k, b, 2, r, sibling)
-        if b >= 2:
-            xcopy(k, b, 5, r, device(x_far, c))
+        xcopy(k, b, 5, r, device(x_far, c))
 
     def x_pass(k, b):
         ring_x[k, b, 0].wait_recv()
-        if b == 0:
-            xcopy(k, b, 5, 2 * x_left + c, device(x_right, c))
         xcopy(k, b, 3, 2 * x_left + c, sibling)
         ring_x[k, b, 1].wait_recv()
-        if b == 1:
-            xcopy(k, b, 5, 2 * x_right + c, device(x_left, c))
         xcopy(k, b, 4, 2 * x_right + c, sibling)
 
     def x_far_pass(k, b):

time: 78.9 us -> 76.9 us (0.975)
  Pallas kernels: 78.2 us -> 76.1 us
    pallas_call x1, Pallas kernels: 76.2 us -> 74.1 us  [body(): pl.pallas_call(kernel, out_shape=shapes + (jax.ShapeDtypeStruct((2, 8, 16...]
where the time goes in v10:
time: 76.9 us; the launch traced here: 76.7 us
  Pallas kernels  76.1 us (99%)
    pallas_call x1, Pallas kernels, body(): pl.pallas_call(kernel, out_shape=shapes + (jax.ShapeDtypeStruct((2, 8, 16...  74.1 us
    pallas_call x1, Pallas kernels, body(): pl.pallas_call(finish, out_shape=shapes + (jax.ShapeDtypeStruct((3 * HD,...  1.97 us

profile of v10, /device:TPU:1, one launch (start us, length us, event | category | flops | bytes accessed | tf_op | source)
XLA Modules:
  0.0 76.7 jit_solution(16777062005603607921)
XLA Ops:
  0.6 74.1 %layer.1 = (bf16[128,512]{1,0:T(8,128)(2,1)}, bf16[128,512]{1,0:T(8,128)(2,1)}, bf16[2,8,16,512]{3,2,1,0:T(8,128)(2,1)}) custom-call(f32[8]{0:T(128)} %bias_ref.1, bf16[128,512]{1,0:T(8,128)(2,1)} %bitcast.6, bf16[128,512]{1,0:T(8,128)(2,1)} %bitcast.7, bf16[512,1536]{1,0:T(8,128)(2,1)} %wqkv_hbm.1, bf16[512,512]{1,0:T(8,128)(2,1)} %wout_hbm.1, ...), custom_call_target="tpu_custom_call" | custom-call | tf_op jit(solution)/shard_map/layer/pallas_call | solution.py:637
  74.8 2.0 %finish.1 = (bf16[128,512]{1,0:T(8,128)(2,1)}, bf16[128,512]{1,0:T(8,128)(2,1)}, f32[192,512]{1,0:T(8,128)}, f32[64,512]{1,0:T(8,128)}) custom-call(bf16[128,512]{1,0:T(8,128)(2,1)} %get-tuple-element.11.out_in, bf16[128,512]{1,0:T(8,128)(2,1)} %get-tuple-element.12.gtok_in, bf16[2,8,16,512]{3,2,1,0:T(8,128)(2,1)} %get-tuple-element.13.fin_ref), custom_call_target="tpu_custom_call" | custom-call | tf_op jit(solution)/shard_map/finish/pallas_call | solution.py:648
